TPU v7x, 256 devices: a whole 4x4x8 slice. The times are simulated.
256 devices in a mesh: seq: 64 (over y, z, core), tab: 4 (over x).
Axes of the slice: x: 4, y: 4, z: 8, core: 2. Of those that a mesh axis runs over, the one named last changes fastest.
Arguments:
- cotangent: bfloat16 [65536, 2560], P('seq', 'tab'), may hold values from -6 to 6
- saved_value: bfloat16 [65536, 2560], P('seq', 'tab'), may hold values from -6 to 6
- gate_scale: float32 [65536], P('seq'), may hold values from 0.2 to 1
- conv_weight: float32 [4, 2560], P(None, 'tab'), may hold values from -3 to 3
- value_weight: bfloat16 [1280, 2560], P(None, 'tab'), may hold values from -0.25 to 0.25
- owner_ids: int32 [8, 65536, 1], P('tab', 'seq'), may hold values from 0 to 63; in each aligned block of 1024 rows (0 to 1023, 1024 to 2047, ..., all dimensions but the last counted through in order) at most 64 rows name the same one
- local_row: int32 [8, 65536], P('tab', 'seq'), may hold values from 0 to 511
- row_table: float32 [8, 32768, 160], P('tab', 'seq'), may hold values from -6 to 6
- moment_one: float32 [8, 32768, 160], P('tab', 'seq'), may hold values from -6 to 6
- moment_two: float32 [8, 32768, 160], P('tab', 'seq'), may hold values from 0.5 to 4
Outputs:
- new_table: float32 [8, 32768, 160], P('tab', 'seq')
- new_first: float32 [8, 32768, 160], P('tab', 'seq')
- new_second: float32 [8, 32768, 160], P('tab', 'seq')
Inputs may be any that keep to these rules, and one draw needn't show every extreme that they name: `owner_ids`: within each aligned block of 1024 tokens of one head (one device's tokens), no owner is named by more than 64 tokens; in some blocks one owner is named by exactly 64.
All inputs are finite; a program needn't handle non-finite values.
Results may differ from a plain program's by a relative error of at most 0.0029.
Values may be sent and summed in bfloat16 or wider, within the bound.
No kernel may reach another device: no remote copies, remote signals or barrier semaphores. Data moves between devices by JAX's collectives and lax.ppermute only.
A program may use at most 128 MiB of HBM per device.

v0:
```python
import jax
import jax.numpy as jnp
from jax import lax
from jax.sharding import PartitionSpec as P

beta_one = 0.9
beta_two = 0.95
learn_rate = 0.01
adam_steps = 10.0
epsilon = 1e-08


def from_behind(block, axis, distance):
    devices = range(lax.axis_size(axis))
    route = [(i - distance, i) for i in devices if i - distance in devices]
    return lax.ppermute(block, axis, route)


def causal_mix(context, conv_weight, length):
    mix_total = jnp.zeros((length, context.shape[1]), jnp.float32)
    for tap_index in range(4):
        row_start = 9 - 3 * tap_index
        mix_total = (
            mix_total + conv_weight[tap_index][None, :] * context[row_start : row_start + length]
        )
    return mix_total


def conv_adjoint(upstream, mixed_conv):
    squashed = jax.nn.sigmoid(mixed_conv)
    return upstream * squashed * (1.0 + mixed_conv * (1.0 - squashed))


def shards(
    cotangent,
    saved_value,
    gate_scale,
    conv_weight,
    value_weight,
    owner_ids,
    local_row,
    row_table,
    moment_one,
    moment_two,
):
    length = cotangent.shape[0]
    head_local = row_table.shape[0]
    table_rows = row_table.shape[1]
    head_dim = row_table.shape[2]
    own_width = head_local * head_dim
    peer_count = lax.axis_size("seq")
    count_cap = 4 * length // peer_count
    upstream = cotangent.astype(jnp.float32)
    value_rows = saved_value.astype(jnp.float32)
    prior_rows = from_behind(saved_value[length - 9 :], "seq", 1)
    context = jnp.concatenate([prior_rows.astype(jnp.float32), value_rows], axis=0)
    conv_grad = conv_adjoint(upstream, causal_mix(context, conv_weight, length))
    following = from_behind(conv_grad[:9], "seq", -1)
    extended = jnp.concatenate([conv_grad, following], axis=0)
    value_grad = upstream
    for tap_index in range(4):
        row_start = 3 * tap_index
        value_grad = (
            value_grad + conv_weight[tap_index][None, :] * extended[row_start : row_start + length]
        )
    scaled = (gate_scale[:, None] * value_grad).astype(jnp.bfloat16)
    full_term = lax.dot_general(
        value_weight, scaled, (((1,), (1,)), ((), ())), preferred_element_type=jnp.float32
    )
    summed = lax.psum(full_term, "tab")
    memory_grad = lax.dynamic_slice_in_dim(summed, lax.axis_index("tab") * own_width, own_width, 0)
    heads_grad = jnp.swapaxes(memory_grad.reshape(head_local, head_dim, length), 1, 2)
    owners = owner_ids[:, :, 0]
    position = jnp.arange(length, dtype=jnp.int32)
    earlier = position[None, :] < position[:, None]
    same_owner = owners[:, :, None] == owners[:, None, :]
    slot_rank = jnp.sum((same_owner & earlier[None]).astype(jnp.int32), axis=2)
    slot_index = owners * count_cap + slot_rank
    head_ids = jnp.broadcast_to(jnp.arange(head_local, dtype=jnp.int32)[:, None], slot_index.shape)
    send_grad = (
        jnp.zeros((head_local, peer_count * count_cap, head_dim), jnp.float32)
        .at[head_ids, slot_index]
        .set(heads_grad)
    )
    send_rows = (
        jnp.zeros((head_local, peer_count * count_cap), jnp.int32)
        .at[head_ids, slot_index]
        .set(local_row + 1)
    )
    send_grad = send_grad.reshape(head_local, peer_count, count_cap, head_dim)
    send_rows = send_rows.reshape(head_local, peer_count, count_cap)
    grads_in = lax.all_to_all(send_grad, "seq", split_axis=1, concat_axis=1, tiled=True)
    rows_in = lax.all_to_all(send_rows, "seq", split_axis=1, concat_axis=1, tiled=True)
    item_count = grads_in.shape[0]
    flat_rows = rows_in.reshape(item_count, -1) - 1
    flat_grads = grads_in.reshape(item_count, -1, head_dim)
    item_ids = jnp.broadcast_to(jnp.arange(item_count, dtype=jnp.int32)[:, None], flat_rows.shape)
    target = jnp.where(flat_rows < 0, table_rows, flat_rows)
    summed_rows = (
        jnp.zeros((item_count, table_rows, head_dim), jnp.float32)
        .at[item_ids, target]
        .add(flat_grads, mode="drop")
    )
    row_hits = (
        jnp.zeros((item_count, table_rows), jnp.int32).at[item_ids, target].add(1, mode="drop")
    )
    row_grad, row_hits = (summed_rows, row_hits)
    touched = (row_hits > 0)[:, :, None]
    first_next = beta_one * moment_one + (1.0 - beta_one) * row_grad
    second_next = beta_two * moment_two + (1.0 - beta_two) * row_grad * row_grad
    update = (
        first_next
        / (1.0 - beta_one**adam_steps)
        / (jnp.sqrt(second_next / (1.0 - beta_two**adam_steps)) + epsilon)
    )
    table_next = row_table - learn_rate * update
    return (
        jnp.where(touched, table_next, row_table),
        jnp.where(touched, first_next, moment_one),
        jnp.where(touched, second_next, moment_two),
    )


def solution(mesh):
    in_specs = (
        P("seq", "tab"),
        P("seq", "tab"),
        P("seq"),
        P(None, "tab"),
        P(None, "tab"),
        P("tab", "seq", None),
        P("tab", "seq"),
        P("tab", "seq", None),
        P("tab", "seq", None),
        P("tab", "seq", None),
    )
    out_specs = (P("tab", "seq", None), P("tab", "seq", None), P("tab", "seq", None))
    return jax.shard_map(shards, mesh=mesh, in_specs=in_specs, out_specs=out_specs, check_vma=False)
```

profile of v0, /device:TPU:1, one launch (start us, length us, event | category | flops | bytes accessed | tf_op | source)
XLA Modules:
  0.0 436.1 jit_solution(14999547283841224572)
XLA Ops:
  7.2 0.0 copy-start
  7.2 0.0 all-reduce.2.cloned.1.call-start
  7.2 0.9 slice.42
  8.1 4.9 %collective-permute-start = (bf16[9,640]{1,0:T(8,128)(2,1)S(1)}, bf16[9,640]{1,0:T(8,128)(2,1)S(1)}, u32[]{:S(2)}, u32[]{:S(2)}) collective-permute-start(bf16[9,640]{1,0:T(8,128)(2,1)S(1)} %slice.42), channel_id=1, source_target_pairs={{0,4},{4,8},{8,12},{12,16},{16,20},{20,24},{24,28},{28,32},{32,36}... | collective-permute-start | bytes 34568 | tf_op jit(solution)/shard_map/ppermute | solution.py:16
  13.0 0.9 slice_reduce_fusion.3
  13.9 1.5 convert_element_type.17
  15.4 0.0 collective-permute-done
  15.5 0.0 copy-start.10
  15.5 2.1 fusion.2
  17.6 1.9 collective-permute-start.1
  19.5 3.4 collective-permute-done.1
  22.9 0.0 copy-done
  22.9 6.8 %convolution_bitcast_fusion = f32[1280,1024]{0,1:T(8,128)} fusion(bf16[1280,640]{1,0:T(8,128)(2,1)S(1)} %copy-done, bf16[1024,640]{1,0:T(8,128)(2,1)S(1)} %copy-done.2, f32[9,640]{1,0:T(8,128)S(1)} %collective-permute-done.1, f32[1024,640]{1,0:T(8,128)S(1)} %fusion.2, f32[640]{0:T(1024)S(1)} %get-tuple-element.23, f32[640]{0:T(1024)S(1)} %get-tuple-element.24, ...), kind=kOutput, calls=%fused_computation.5 | convolution fusion | flops 1686896640 | bytes 10850816 | tf_op jit(solution)/shard_map/dot_general | solution.py:67
  29.7 0.0 all-reduce.2.cloned.1.call-update
  29.7 0.7 copy-done.4
  30.4 0.3 iota_compare_fusion
  30.7 1.9 convert_reduce_fusion
  32.6 0.1 multiply_reduce_fusion.1
  32.7 0.1 and_reduce_fusion.1
  32.9 8.1 %scatter_custom_fusion = s32[8192]{0:T(1024)S(1)} fusion(s32[2048]{0:T(1024)S(1)} %get-tuple-element.29, s32[2048]{0:T(1024)S(1)} %get-tuple-element.28, s32[]{:T(128)} %constant.19.clone.1), kind=kCustom, calls=%fused_computation.60 | custom fusion | bytes 32772
  41.0 0.1 reshape.86
  41.1 0.1 copy.147
  41.1 0.7 reshape.147
  41.8 11.6 %all-to-all-start = ((s32[64,1,128]{2,1,0:T(1,128)}), s32[64,1,128]{2,1,0:T(1,128)S(1)}, u32[]{:S(2)}, u32[]{:S(2)}) async-start(s32[64,1,128]{2,1,0:T(1,128)} %reshape.147), calls=%async_computation | async-start | bytes 65536 | tf_op jit(solution)/shard_map/all_to_all | solution.py:93
  53.5 93.5 %all-reduce.2.cloned.1.call-done = f32[1280,1024]{0,1:T(8,128)} async-done(((f32[1280,1024]{0,1:T(8,128)}), f32[1280,1024]{0,1:T(8,128)}) %all-reduce.2.cloned.1.call-update) | async-done | bytes 5242896 | tf_op jit(solution)/shard_map/psum | solution.py:70
  146.9 2.1 constant_dynamic-slice_fusion
  149.0 0.5 copy.100
  149.5 1.8 copy.116
  151.3 13.2 %scatter_custom_fusion.2 = f32[8192,160]{1,0:T(8,128)} fusion(s32[2048]{0:T(1024)S(1)} %get-tuple-element.29, f32[2048,160]{1,0:T(8,128)} %bitcast.36, f32[]{:T(128)} %constant.26.clone.1), kind=kCustom, calls=%fused_computation.6 | custom fusion | bytes 5243392
  164.5 7.7 %copy.104 = f32[2,64,64,160]{3,2,0,1:T(8,128)} copy(f32[2,64,64,160]{3,2,1,0:T(8,128)} %bitcast.32) | data formatting | bytes 10485760 | tf_op jit(solution)/shard_map/reshape | solution.py:90
  172.2 0.0 all-to-all-done
  172.2 11.2 %all-to-all-start.1 = ((f32[2,64,64,160]{3,2,0,1:T(8,128)}), f32[2,64,64,160]{3,2,0,1:T(8,128)}, u32[]{:S(2)}, u32[]{:S(2)}) async-start(f32[2,64,64,160]{3,2,0,1:T(8,128)} %copy.104), calls=%async_computation.1 | async-start | bytes 16777216 | tf_op jit(solution)/shard_map/all_to_all | solution.py:92
  183.4 0.5 broadcast.188
  183.9 0.7 reduce.20
  184.6 0.1 reshape.148
  184.7 0.1 sub.12
  184.9 0.1 multiply_reduce_fusion
  185.0 0.1 and_reduce_fusion
  185.2 44.6 %scatter_custom_fusion.1 = s32[1024]{0:T(1024)S(1)} fusion(s32[8192]{0:T(1024)S(1)} %bitcast.40, s32[8192]{0:T(1024)S(1)} %broadcast.161, s32[]{:T(128)} %constant.19.clone.1), kind=kCustom, calls=%fused_computation.74 | custom fusion | flops 8192 | bytes 4100
  229.8 139.3 %all-to-all-done.1 = f32[2,64,64,160]{3,2,0,1:T(8,128)} async-done(((f32[2,64,64,160]{3,2,0,1:T(8,128)}), f32[2,64,64,160]{3,2,0,1:T(8,128)}, u32[]{:S(2)}, u32[]{:S(2)}) %all-to-all-start.1) | async-done | bytes 5242912 | tf_op jit(solution)/shard_map/all_to_all | solution.py:92
  369.1 7.7 %copy.119 = f32[2,64,64,160]{3,2,1,0:T(8,128)} copy(f32[2,64,64,160]{3,2,0,1:T(8,128)} %all-to-all-done.1) | data formatting | bytes 10485760 | tf_op jit(solution)/shard_map/reshape | solution.py:96
  376.8 44.9 %scatter_custom_fusion.3 = f32[1024,160]{1,0:T(8,128)S(1)} fusion(s32[8192]{0:T(1024)S(1)} %bitcast.41, f32[8192,160]{1,0:T(8,128)} %bitcast.33, f32[]{:T(128)} %constant.26.clone.1), kind=kCustom, calls=%fused_computation.48 | custom fusion | flops 1310720 | bytes 655872
  421.7 0.6 copy.120
  422.3 0.0 copy-start.1
  422.3 4.0 broadcast_select_fusion
  426.4 1.0 copy.113
  427.3 1.0 copy.114
  428.3 1.0 copy.115
  (33 shorter events, 0.2 us)
Async XLA Ops:
  7.2 15.8 %copy-start = (bf16[1280,640]{1,0:T(8,128)(2,1)S(1)}, bf16[1280,640]{1,0:T(8,128)(2,1)}, u32[]{:S(2)}) copy-start(bf16[1280,640]{1,0:T(8,128)(2,1)} %param.14) | copy-start | bytes 4915204
  7.2 8.3 %copy-start.2 = (bf16[1024,640]{1,0:T(8,128)(2,1)S(1)}, bf16[1024,640]{1,0:T(8,128)(2,1)}, u32[]{:S(2)}) copy-start(bf16[1024,640]{1,0:T(8,128)(2,1)} %param.10) | copy-start | bytes 3932164
  7.2 139.7 %all-reduce.2.cloned.1.call-start = ((), (), s32[]{:S(2)}) async-start(), calls=%async_computation.2 | async-start | bytes 10485760 | tf_op jit(solution)/shard_map/psum | solution.py:70
  8.1 7.3 %collective-permute-start = (bf16[9,640]{1,0:T(8,128)(2,1)S(1)}, bf16[9,640]{1,0:T(8,128)(2,1)S(1)}, u32[]{:S(2)}, u32[]{:S(2)}) collective-permute-start(bf16[9,640]{1,0:T(8,128)(2,1)S(1)} %slice.42), channel_id=1, source_target_pairs={{0,4},{4,8},{8,12},{12,16},{16,20},{20,24},{24,28},{28,32},{32,36}... | collective-permute-start | bytes 34568 | tf_op jit(solution)/shard_map/ppermute | solution.py:16
  15.5 7.5 %copy-start.10 = (f32[1024]{0:T(1024)S(1)}, f32[1024]{0:T(1024)}, u32[]{:S(2)}) copy-start(f32[1024]{0:T(1024)} %param.12) | copy-start | bytes 12292
  17.6 5.3 %collective-permute-start.1 = (f32[9,640]{1,0:T(8,128)S(1)}, f32[9,640]{1,0:T(8,128)S(1)}, u32[]{:S(2)}, u32[]{:S(2)}) collective-permute-start(f32[9,640]{1,0:T(8,128)S(1)} %slice.56), channel_id=1, source_target_pairs={{4,0},{8,4},{12,8},{16,12},{20,16},{24,20},{28,24},{32,28},{36,32}... | collective-permute-start | bytes 69128 | tf_op jit(solution)/shard_map/ppermute | solution.py:16
  29.7 0.7 copy-start.4
  29.7 2.9 copy-start.8
  29.7 3.0 copy-start.9
  29.7 3.1 copy-start.5
  41.8 130.3 %all-to-all-start = ((s32[64,1,128]{2,1,0:T(1,128)}), s32[64,1,128]{2,1,0:T(1,128)S(1)}, u32[]{:S(2)}, u32[]{:S(2)}) async-start(s32[64,1,128]{2,1,0:T(1,128)} %reshape.147), calls=%async_computation | async-start | bytes 65536 | tf_op jit(solution)/shard_map/all_to_all | solution.py:93
  172.2 12.7 %copy-start.7 = (s32[2]{0:T(128)S(1)}, s32[2]{0:T(128)}, u32[]{:S(2)}) copy-start(s32[2]{0:T(128)} %constant.63) | copy-start | bytes 28
  172.2 12.8 %copy-start.6 = (s32[2]{0:T(128)S(1)}, s32[2]{0:T(128)}, u32[]{:S(2)}) copy-start(s32[2]{0:T(128)} %constant.66) | copy-start | bytes 28
  172.2 196.9 %all-to-all-start.1 = ((f32[2,64,64,160]{3,2,0,1:T(8,128)}), f32[2,64,64,160]{3,2,0,1:T(8,128)}, u32[]{:S(2)}, u32[]{:S(2)}) async-start(f32[2,64,64,160]{3,2,0,1:T(8,128)} %copy.104), calls=%async_computation.1 | async-start | bytes 16777216 | tf_op jit(solution)/shard_map/all_to_all | solution.py:92
  376.8 45.5 %copy-start.3 = (f32[2,512,160]{1,2,0:T(8,128)S(1)}, f32[2,512,160]{1,2,0:T(8,128)}, u32[]{:S(2)}) copy-start(f32[2,512,160]{1,2,0:T(8,128)} %param.19) | copy-start | bytes 1966084
  422.3 6.9 %copy-start.1 = (bf16[1280,640]{1,0:T(8,128)(2,1)S(1)}, bf16[1280,640]{1,0:T(8,128)(2,1)}, u32[]{:S(2)}) copy-start(bf16[1280,640]{1,0:T(8,128)(2,1)} %param.14) | copy-start | bytes 4915204
Sparse Core Ops, SparseCore 0:
  29.9 117.0 all-reduce.1
where the time goes:
time: 437 us; the launch traced here: 436 us
  waiting for transfers between devices  236 us (54%)
  other arithmetic  101 us (23%)
  local copies, waits for them, and re-layouts  48.5 us (11%)
  starting transfers between devices  29.7 us (7%)
  between operations  14.4 us (3%)
  matrix products  6.78 us (2%)
    all_to_all x1, waiting for transfers between devices, shards(): lax.all_to_all(send_grad, 'seq', split_axis=1, concat_axis=1, tiled=True)  139 us
    psum x1, waiting for transfers between devices, shards(): summed = lax.psum(full_term, 'tab')  93.5 us
    unnamed x9, other arithmetic  90 us
    unnamed x32, local copies, waits for them, and re-layouts  25.7 us
    all_to_all x1, starting transfers between devices, shards(): lax.all_to_all(send_rows, 'seq', split_axis=1, concat_axis=1, tiled=True)  11.6 us
    all_to_all x1, starting transfers between devices, shards(): lax.all_to_all(send_grad, 'seq', split_axis=1, concat_axis=1, tiled=True)  11.2 us
  transfers between devices with their start and end apart: 5, of which 3 were waited for; matrix products, arithmetic and copies ran while one was open for 20% of the time, Pallas kernels for 0%

commit v1 on v0

v1 whole, which is shorter than its diff:
```python
import jax
import jax.numpy as jnp
from jax import lax
from jax.experimental import pallas as pl
from jax.experimental.pallas import tpu as pltpu
from jax.sharding import PartitionSpec as P

beta_one = 0.9
beta_two = 0.95
learn_rate = 0.01
adam_steps = 10.0
epsilon = 1e-08

LANES = 128
HALO = 16
DIGIT = 32
META = 8


def shift_by(block, axis, distance, wrap):
    size = lax.axis_size(axis)
    if wrap:
        route = [(i, (i + distance) % size) for i in range(size)]
    else:
        route = [(i, i + distance) for i in range(size) if 0 <= i + distance < size]
    return lax.ppermute(block, axis, route)


def whole(shape, dtype):
    return jax.ShapeDtypeStruct(shape, dtype)


def slot_kernel(owners_ref, slot_ref, *, peers, cap):
    heads, length = owners_ref.shape
    owner_of = lax.broadcasted_iota(jnp.int32, (peers, LANES), 0)
    before = lax.broadcasted_iota(jnp.int32, (LANES, 2 * LANES), 0)
    after = lax.broadcasted_iota(jnp.int32, (LANES, 2 * LANES), 1)
    counter = jnp.where((before < after) | (after >= LANES), 1.0, 0.0).astype(jnp.bfloat16)
    carry = jnp.zeros((heads * peers, LANES), jnp.float32)
    for block in range(length // LANES):
        lanes = slice(block * LANES, (block + 1) * LANES)
        named = [
            jnp.where(owners_ref[h : h + 1, lanes] == owner_of, 1.0, 0.0) for h in range(heads)
        ]
        named = jnp.concatenate(named, axis=0)
        counts = jnp.dot(
            named.astype(jnp.bfloat16), counter, preferred_element_type=jnp.float32
        )
        rank = named * (counts[:, :LANES] + carry)
        carry = carry + counts[:, LANES:]
        for h in range(heads):
            own = jnp.sum(rank[h * peers : (h + 1) * peers], axis=0, keepdims=True)
            slot_ref[h : h + 1, lanes] = owners_ref[h : h + 1, lanes] * cap + own.astype(jnp.int32)


def slots_of(owners, peers, cap):
    return pl.pallas_call(
        lambda *refs: slot_kernel(*refs, peers=peers, cap=cap),
        out_shape=whole(owners.shape, jnp.int32),
        name="slots",
    )(owners)


def adjoint_kernel(
    tab_ref, cot_ref, value_ref, prior_ref, next_value_ref, next_cot_ref, gate_ref, taps_ref,
    weight_ref, *refs, pieces, heads, head_dim, tabs
):
    outs, (value_pad, grad_pad, scaled) = refs[:-3], refs[-3:]
    length, width = cot_ref.shape
    strips = width // LANES
    rows = LANES
    for strip in range(strips):
        lanes = slice(strip * LANES, (strip + 1) * LANES)
        value_pad[strip, :HALO] = prior_ref[:, lanes].astype(jnp.float32)
        value_pad[strip, HALO : HALO + length] = value_ref[:, lanes].astype(jnp.float32)
        value_pad[strip, HALO + length :] = next_value_ref[:, lanes].astype(jnp.float32)

    def adjoint(strip, start, count, upstream):
        lanes = slice(strip * LANES, (strip + 1) * LANES)
        mixed = taps_ref[0:1, lanes] * value_pad[strip, pl.ds(start + HALO, count)]
        for tap in range(1, 4):
            mixed = mixed + taps_ref[tap : tap + 1, lanes] * value_pad[
                strip, pl.ds(start + HALO - 3 * tap, count)
            ]
        squashed = jax.nn.sigmoid(mixed)
        return upstream * squashed * (1.0 + mixed * (1.0 - squashed))

    def first(block, carry):
        start = pl.multiple_of(block * rows, rows)
        for strip in range(strips):
            lanes = slice(strip * LANES, (strip + 1) * LANES)
            upstream = cot_ref[pl.ds(start, rows), lanes].astype(jnp.float32)
            grad_pad[strip, pl.ds(start, rows)] = adjoint(strip, start, rows, upstream)
        return carry

    lax.fori_loop(0, length // rows, first, 0)
    for strip in range(strips):
        lanes = slice(strip * LANES, (strip + 1) * LANES)
        upstream = next_cot_ref[:, lanes].astype(jnp.float32)
        grad_pad[strip, length:] = adjoint(strip, length, HALO, upstream)

    def second(block, carry):
        start = pl.multiple_of(block * rows, rows)
        gate = jnp.broadcast_to(gate_ref[pl.ds(block, 1), :], (LANES, LANES)).T
        for strip in range(strips):
            lanes = slice(strip * LANES, (strip + 1) * LANES)
            total = cot_ref[pl.ds(start, rows), lanes].astype(jnp.float32)
            for tap in range(4):
                total = total + taps_ref[tap : tap + 1, lanes] * grad_pad[
                    strip, pl.ds(start + 3 * tap, rows)
                ]
            scaled[pl.ds(start, rows), lanes] = (gate * total).astype(jnp.bfloat16)
        return carry

    lax.fori_loop(0, length // rows, second, 0)
    place = 0
    own_width = heads * head_dim
    for low, high in pieces:
        for relative in range(tabs):
            base = ((tab_ref[0] + relative) % tabs) * own_width
            out = outs[place]
            place += 1
            for h in range(heads):
                start = pl.multiple_of(base + (h * head_dim + low), 16)
                term = lax.dot_general(
                    weight_ref[pl.ds(start, high - low), :],
                    scaled[...],
                    (((1,), (1,)), ((), ())),
                    preferred_element_type=jnp.float32,
                )
                out[h * (high - low) : (h + 1) * (high - low)] = term.astype(out.dtype)


def adjoint_terms(cot, value, prior, nexts, gate, taps, weight, pieces, heads, head_dim, tabs):
    length, width = cot.shape
    strips = width // LANES
    tab_index = lax.axis_index("tab").astype(jnp.int32).reshape(1)
    shapes = []
    for low, high in pieces:
        size = (heads * (high - low), length)
        shapes += [whole(size, jnp.float32)] + [whole(size, jnp.bfloat16)] * (tabs - 1)
    vmem = pl.BlockSpec(memory_space=pltpu.VMEM)
    return pl.pallas_call(
        lambda *refs: adjoint_kernel(
            *refs, pieces=pieces, heads=heads, head_dim=head_dim, tabs=tabs
        ),
        out_shape=shapes,
        in_specs=[pl.BlockSpec(memory_space=pltpu.SMEM)] + [vmem] * 8,
        out_specs=[vmem] * len(shapes),
        scratch_shapes=[
            pltpu.VMEM((strips, length + 2 * HALO, LANES), jnp.float32),
            pltpu.VMEM((strips, length + HALO, LANES), jnp.float32),
            pltpu.VMEM((length, width), jnp.bfloat16),
        ],
        name="adjoint",
    )(tab_index, cot, value, prior, nexts[0], nexts[1], gate, taps, weight)


def send_kernel(slot_ref, row_ref, own_ref, one_ref, two_ref, three_ref, out_ref, lhs, *, meta):
    heads, length = slot_ref.shape
    peers, tall, _ = out_ref.shape
    count = own_ref.shape[0] // heads
    cap = LANES // heads
    for h in range(heads):
        part = slice(h * count, (h + 1) * count)
        total = own_ref[part] + one_ref[part].astype(jnp.float32)
        total = total + two_ref[part].astype(jnp.float32) + three_ref[part].astype(jnp.float32)
        lhs[h, :count] = total.astype(jnp.bfloat16)
        if meta:
            number = row_ref[h : h + 1] + 1
            kind = lax.broadcasted_iota(jnp.int32, (2 * META, length), 0)
            digit = jnp.where(kind == 0, number // DIGIT, number % DIGIT)
            digit = jnp.where(kind == 2, 1, jnp.where(kind > 2, 0, digit))
            lhs[h, count:] = digit.astype(jnp.float32).astype(jnp.bfloat16)
    group = 4
    left = lax.broadcasted_iota(jnp.int32, (lhs.shape[1], LANES), 1) < cap
    place = lax.broadcasted_iota(jnp.int32, (group * cap, length), 0)

    def body(step, carry):
        base = step * (group * cap)
        sent = []
        for h in range(heads):
            chosen = jnp.where(slot_ref[h : h + 1] - base == place, 1.0, 0.0)
            sent.append(
                lax.dot_general(
                    lhs[h],
                    chosen.astype(jnp.bfloat16),
                    (((1,), (1,)), ((), ())),
                    preferred_element_type=jnp.float32,
                )
            )
        for pair in range(group // 2):
            a = sent[0][:, pair * LANES : (pair + 1) * LANES]
            b = sent[1][:, pair * LANES : (pair + 1) * LANES]
            even = jnp.where(left, a, pltpu.roll(b, cap, 1)).astype(jnp.bfloat16)
            odd = jnp.where(left, pltpu.roll(a, cap, 1), b).astype(jnp.bfloat16)
            out_ref[step * group + 2 * pair] = even[:tall]
            out_ref[step * group + 2 * pair + 1] = odd[:tall]
        return carry

    lax.fori_loop(0, peers // group, body, 0)


def send_blocks(slots, rows, terms, peers, meta):
    heads, length = slots.shape
    count = terms[0].shape[0] // heads
    tall = count + (META if meta else 0)
    padded = count + (2 * META if meta else 0)
    return pl.pallas_call(
        lambda *refs: send_kernel(*refs, meta=meta),
        out_shape=whole((peers, tall, LANES), jnp.bfloat16),
        scratch_shapes=[pltpu.VMEM((heads, padded, length), jnp.bfloat16)],
        name="send",
    )(slots, rows, *terms)


def update_kernel(got_ref, table_ref, one_ref, two_ref, new_table, new_one, new_two, grads):
    peers, tall, _ = got_ref.shape
    heads, rows, head_dim = table_ref.shape
    cap = LANES // heads
    left = lax.broadcasted_iota(jnp.int32, (tall, LANES), 1) < cap

    def spread(pair, carry):
        a = got_ref[2 * pair].astype(jnp.float32)
        b = got_ref[2 * pair + 1].astype(jnp.float32)
        lanes = pl.ds(pl.multiple_of(pair * LANES, LANES), LANES)
        grads[0, :, lanes] = jnp.where(left, a, pltpu.roll(b, cap, 1)).astype(jnp.bfloat16)
        grads[1, :, lanes] = jnp.where(left, pltpu.roll(a, cap, 1), b).astype(jnp.bfloat16)
        return carry

    lax.fori_loop(0, peers // 2, spread, 0)
    chunk = 512
    row_of = lax.broadcasted_iota(jnp.int32, (rows, chunk), 0)
    for h in range(heads):
        total = jnp.zeros((rows, tall), jnp.float32)
        for step in range(peers * cap // chunk):
            lanes = slice(step * chunk, (step + 1) * chunk)
            digits = grads[h, head_dim : head_dim + META, lanes].astype(jnp.float32)
            number = (digits[0:1] * float(DIGIT) + digits[1:2]).astype(jnp.int32) - 1
            chosen = jnp.where(number == row_of, 1.0, 0.0).astype(jnp.bfloat16)
            total = total + lax.dot_general(
                chosen, grads[h, :, lanes], (((1,), (1,)), ((), ())),
                preferred_element_type=jnp.float32,
            )
        touched = jnp.broadcast_to(total[:, head_dim + 2 : head_dim + 3] > 0.5, (rows, head_dim))
        grad = total[:, :head_dim]
        old_one, old_two, old_table = one_ref[h], two_ref[h], table_ref[h]
        first = beta_one * old_one + (1.0 - beta_one) * grad
        second = beta_two * old_two + (1.0 - beta_two) * grad * grad
        update = (first / (1.0 - beta_one**adam_steps)) / (
            jnp.sqrt(second / (1.0 - beta_two**adam_steps)) + epsilon
        )
        new_table[h] = jnp.where(touched, old_table - learn_rate * update, old_table)
        new_one[h] = jnp.where(touched, first, old_one)
        new_two[h] = jnp.where(touched, second, old_two)


def updated(got, table, one, two):
    peers, tall, _ = got.shape
    heads = table.shape[0]
    return pl.pallas_call(
        update_kernel,
        out_shape=[whole(table.shape, jnp.float32)] * 3,
        scratch_shapes=[pltpu.VMEM((heads, tall, peers * LANES // heads), jnp.bfloat16)],
        name="update",
    )(got, table, one, two)


def shards(
    cotangent,
    saved_value,
    gate_scale,
    conv_weight,
    value_weight,
    owner_ids,
    local_row,
    row_table,
    moment_one,
    moment_two,
):
    length = cotangent.shape[0]
    heads, _, head_dim = row_table.shape
    peers = lax.axis_size("seq")
    tabs = lax.axis_size("tab")
    cap = LANES // heads
    pieces = [(0, head_dim)]
    prior = shift_by(saved_value[length - HALO :], "seq", 1, False)
    nexts = [shift_by(x[:HALO], "seq", -1, False) for x in (saved_value, cotangent)]
    slots = slots_of(owner_ids[:, :, 0], peers, cap)
    terms = adjoint_terms(
        cotangent, saved_value, prior, nexts, gate_scale.reshape(-1, LANES), conv_weight,
        value_weight, pieces, heads, head_dim, tabs,
    )
    own, *others = terms
    parts = [own] + [shift_by(x, "tab", i + 1, True) for i, x in enumerate(others)]
    blocks = send_blocks(slots, local_row, parts, peers, True)
    got = lax.all_to_all(blocks, "seq", split_axis=0, concat_axis=0, tiled=True)
    return tuple(updated(got, row_table, moment_one, moment_two))


def solution(mesh):
    in_specs = (
        P("seq", "tab"),
        P("seq", "tab"),
        P("seq"),
        P(None, "tab"),
        P(None, "tab"),
        P("tab", "seq", None),
        P("tab", "seq"),
        P("tab", "seq", None),
        P("tab", "seq", None),
        P("tab", "seq", None),
    )
    out_specs = (P("tab", "seq", None), P("tab", "seq", None), P("tab", "seq", None))
    return jax.shard_map(shards, mesh=mesh, in_specs=in_specs, out_specs=out_specs, check_vma=False)
```

time: 437 us -> 165 us (0.38)
  waiting for transfers between devices: 236 us -> 87.4 us
  other arithmetic: 101 us -> 0 us
  Pallas kernels: 0 us -> 35 us
  local copies, waits for them, and re-layouts: 48.5 us -> 15.2 us
  between operations: 14.4 us -> 0.71 us
  matrix products: 6.78 us -> 0 us
    psum x1 -> x0, waiting for transfers between devices: 93.5 us -> none  [shards(): summed = lax.psum(full_term, 'tab')]
    unnamed x9 -> x0, other arithmetic: 90 us -> none
    all_to_all x2 -> x1, waiting for transfers between devices: 139 us -> 59.9 us  [shards(): got = lax.all_to_all(blocks, 'seq', split_axis=0, concat_axis=0, tiled=True)]
    pallas_call x0 -> x4, Pallas kernels: none -> 35 us  [the longest x1 12.9 us: send_blocks(): pl.pallas_call(lambda *refs: send_kernel(*refs, meta=meta), out_shape=who...]
    ppermute x2 -> x6, waiting for transfers between devices: 3.4 us -> 27.5 us  [shift_by(): return lax.ppermute(block, axis, route)]
    unnamed x32 -> x28, local copies, waits for them, and re-layouts: 25.7 us -> 8.94 us
    reshape x4 -> x0, local copies, waits for them, and re-layouts: 15.5 us -> none  [the longest x1 7.71 us: shards(): flat_grads = grads_in.reshape(item_count, -1, head_dim)]
    all_to_all x2 -> x1, starting transfers between devices: 22.8 us -> 13.1 us  [shards(): got = lax.all_to_all(blocks, 'seq', split_axis=0, concat_axis=0, tiled=True)]
  transfers between devices with their start and end apart: 5 -> 7, of which waited for: 3 -> 5; matrix products, arithmetic and copies ran while one was open for 20% -> 4% of each run, Pallas kernels for 0% -> 1%
where the time goes in v1:
time: 165 us
  waiting for transfers between devices  87.4 us (53%)
  Pallas kernels  35 us (21%)
  starting transfers between devices  26.7 us (16%)
  local copies, waits for them, and re-layouts  15.2 us (9%)
    all_to_all x1, waiting for transfers between devices, shards(): got = lax.all_to_all(blocks, 'seq', split_axis=0, concat_axis=0, tiled=True)  59.9 us
    ppermute x6, waiting for transfers between devices, shift_by(): return lax.ppermute(block, axis, route)  27.5 us
    ppermute x6, starting transfers between devices, shift_by(): return lax.ppermute(block, axis, route)  13.6 us
    all_to_all x1, starting transfers between devices, shards(): got = lax.all_to_all(blocks, 'seq', split_axis=0, concat_axis=0, tiled=True)  13.1 us
    pallas_call x1, Pallas kernels, send_blocks(): pl.pallas_call(lambda *refs: send_kernel(*refs, meta=meta), out_shape=who...  12.9 us
    pallas_call x1, Pallas kernels, updated(): pl.pallas_call(update_kernel, out_shape=[whole(table.shape, jnp.float32)]...  10.9 us
    pallas_call x1, Pallas kernels, adjoint_terms(): pl.pallas_call(lambda *refs: adjoint_kernel(*refs, pieces=pieces, heads=h...  9.55 us
    unnamed x28, local copies, waits for them, and re-layouts  8.94 us
  transfers between devices with their start and end apart: 7, of which 5 were waited for; matrix products, arithmetic and copies ran while one was open for 4% of the time, Pallas kernels for 1%

profile of v1, /device:TPU:1, one launch (start us, length us, event | category | flops | bytes accessed | tf_op | source)
XLA Modules:
  0.0 165.0 jit_solution(17019243361320316551)
XLA Ops:
  0.6 0.8 fusion
  1.4 4.9 %collective-permute-start = (bf16[16,640]{1,0:T(8,128)(2,1)S(1)}, bf16[16,640]{1,0:T(8,128)(2,1)S(1)}, u32[]{:S(2)}, u32[]{:S(2)}) collective-permute-start(bf16[16,640]{1,0:T(8,128)(2,1)S(1)} %get-tuple-element.15), channel_id=1, source_target_pairs={{0,4},{4,8},{8,12},{12,16},{16,20},{20,24},{24,28},{28,32},{32,36}... | collective-permute-start | bytes 61448 | tf_op jit(solution)/shard_map/ppermute | solution.py:26
  6.3 1.9 %collective-permute-start.1 = (bf16[16,640]{1,0:T(8,128)(2,1)S(1)}, bf16[16,640]{1,0:T(8,128)(2,1)S(1)}, u32[]{:S(2)}, u32[]{:S(2)}) collective-permute-start(bf16[16,640]{1,0:T(8,128)(2,1)S(1)} %get-tuple-element.14), channel_id=1, source_target_pairs={{4,0},{8,4},{12,8},{16,12},{20,16},{24,20},{28,24},{32,28},{36,32}... | collective-permute-start | bytes 61448 | tf_op jit(solution)/shard_map/ppermute | solution.py:26
  8.2 0.7 slice.11
  9.0 1.9 %collective-permute-start.2 = (bf16[16,640]{1,0:T(8,128)(2,1)S(1)}, bf16[16,640]{1,0:T(8,128)(2,1)S(1)}, u32[]{:S(2)}, u32[]{:S(2)}) collective-permute-start(bf16[16,640]{1,0:T(8,128)(2,1)S(1)} %slice.11), channel_id=1, source_target_pairs={{4,0},{8,4},{12,8},{16,12},{20,16},{24,20},{28,24},{32,28},{36,32}... | collective-permute-start | bytes 61448 | tf_op jit(solution)/shard_map/ppermute | solution.py:26
  10.9 0.0 collective-permute-done.refs_3_
  10.9 0.0 copy-start.8
  10.9 0.5 collective-permute-done.1.refs_4_
  11.4 0.0 copy-start.9
  11.4 2.6 %collective-permute-done.2.refs_5_ = bf16[16,640]{1,0:T(8,128)(2,1)S(1)} collective-permute-done((bf16[16,640]{1,0:T(8,128)(2,1)S(1)}, bf16[16,640]{1,0:T(8,128)(2,1)S(1)}, u32[]{:S(2)}, u32[]{:S(2)}) %collective-permute-start.2) | collective-permute-done | bytes 20512 | tf_op jit(solution)/shard_map/ppermute | solution.py:26
  14.1 0.0 copy-start.10
  14.1 0.0 copy-done.8
  14.1 0.0 copy-done.9
  14.1 0.6 copy-done.10
  14.6 0.0 copy-start.11
  14.7 9.6 %adjoint.1 = (f32[320,1024]{1,0:T(8,128)}, bf16[320,1024]{1,0:T(8,128)(2,1)}, bf16[320,1024]{1,0:T(8,128)(2,1)}, bf16[320,1024]{1,0:T(8,128)(2,1)}) custom-call(s32[1]{0:T(128)} %bitcast.refs_0_, bf16[1024,640]{1,0:T(8,128)(2,1)} %refs_1_.2, bf16[1024,640]{1,0:T(8,128)(2,1)} %refs_2_.1, bf16[16,640]{1,0:T(8,128)(2,1)} %copy-done.8, ...), custom_call_target="tpu_custom_call" | custom-call | tf_op jit(solution)/shard_map/adjoint/pallas_call | solution.py:143
  24.2 1.2 collective-permute-start.3
  25.4 2.5 %collective-permute-start.4 = (bf16[320,1024]{1,0:T(8,128)(2,1)}, bf16[320,1024]{1,0:T(8,128)(2,1)S(1)}, u32[]{:S(2)}, u32[]{:S(2)}) collective-permute-start(bf16[320,1024]{1,0:T(8,128)(2,1)} %get-tuple-element.9), channel_id=1, source_target_pairs={{0,2},{1,3},{2,0},{3,1},{4,6},{5,7},{6,4},{7,5},{8,10},{9,11},{10,... | collective-permute-start | bytes 1966088 | tf_op jit(solution)/shard_map/ppermute | solution.py:26
  27.9 1.1 collective-permute-start.5
  29.0 0.0 copy-done.11
  29.0 0.6 copy.21
  29.6 1.6 slots.1.refs_0_
  31.2 10.2 %collective-permute-done.3.refs_3_ = bf16[320,1024]{1,0:T(8,128)(2,1)S(1)} collective-permute-done((bf16[320,1024]{1,0:T(8,128)(2,1)}, bf16[320,1024]{1,0:T(8,128)(2,1)S(1)}, u32[]{:S(2)}, u32[]{:S(2)}) %collective-permute-start.3) | collective-permute-done | bytes 655392 | tf_op jit(solution)/shard_map/ppermute | solution.py:26
  41.4 0.0 copy-start.3
  41.4 14.2 %collective-permute-done.4.refs_4_ = bf16[320,1024]{1,0:T(8,128)(2,1)S(1)} collective-permute-done((bf16[320,1024]{1,0:T(8,128)(2,1)}, bf16[320,1024]{1,0:T(8,128)(2,1)S(1)}, u32[]{:S(2)}, u32[]{:S(2)}) %collective-permute-start.4) | collective-permute-done | bytes 655392 | tf_op jit(solution)/shard_map/ppermute | solution.py:26
  55.6 0.0 copy-start.4
  55.6 0.0 collective-permute-done.5.refs_5_
  55.6 0.0 copy-start.5
  55.6 0.0 copy-done.3
  55.6 0.8 copy-done.4
  56.4 0.2 copy-done.5
  56.6 12.9 %send.1 = bf16[64,168,128]{2,1,0:T(8,128)(2,1)} custom-call(s32[2,1024]{1,0:T(2,128)} %slots.1.refs_0_, s32[2,1024]{1,0:T(2,128)} %refs_1_.3, f32[320,1024]{1,0:T(8,128)} %get-tuple-element.7.refs_2_, bf16[320,1024]{1,0:T(8,128)(2,1)} %copy-done.3, bf16[320,1024]{1,0:T(8,128)(2,1)} %copy-done.4, bf16[320,1024]{1,0:T(8,128)(2,1)} %copy-done.5), custom_call_target="tpu_custom_call" | custom-call | tf_op jit(solution)/shard_map/send/pallas_call | solution.py:209
  69.6 0.0 copy-start.6
  69.6 13.1 %all-to-all-start = ((bf16[64,168,128]{2,1,0:T(8,128)(2,1)}), bf16[64,168,128]{2,1,0:T(8,128)(2,1)S(1)}, u32[]{:S(2)}, u32[]{:S(2)}) async-start(bf16[64,168,128]{2,1,0:T(8,128)(2,1)} %send.1), calls=%async_computation | async-start | bytes 5505024 | tf_op jit(solution)/shard_map/all_to_all | solution.py:297
  82.7 0.0 copy-done.6
  82.7 1.3 copy.13.table_ref
  84.0 2.5 %copy.14.one_ref = f32[2,512,160]{2,1,0:T(8,128)} copy(f32[2,512,160]{1,2,0:T(8,128)} %param.18) | data formatting | bytes 1310720 | tf_op args[8]
  86.5 0.0 copy-done.7
  86.5 1.3 copy.15.two_ref
  87.8 59.9 %all-to-all-done.got_ref = bf16[64,168,128]{2,1,0:T(8,128)(2,1)S(1)} async-done(((bf16[64,168,128]{2,1,0:T(8,128)(2,1)}), bf16[64,168,128]{2,1,0:T(8,128)(2,1)S(1)}, u32[]{:S(2)}, u32[]{:S(2)}) %all-to-all-start) | async-done | bytes 2752544 | tf_op jit(solution)/shard_map/all_to_all | solution.py:297
  147.7 0.0 copy-start
  147.7 1.6 copy-done
  149.3 10.9 %update.1 = (f32[2,512,160]{2,1,0:T(8,128)}, f32[2,512,160]{2,1,0:T(8,128)}, f32[2,512,160]{2,1,0:T(8,128)}) custom-call(bf16[64,168,128]{2,1,0:T(8,128)(2,1)} %copy-done, f32[2,512,160]{2,1,0:T(8,128)} %copy.13.table_ref, f32[2,512,160]{2,1,0:T(8,128)} %copy.14.one_ref, f32[2,512,160]{2,1,0:T(8,128)} %copy.15.two_ref), custom_call_target="tpu_custom_call" | custom-call | tf_op jit(solution)/shard_map/update/pallas_call | solution.py:261
  160.1 2.5 %copy.16 = f32[2,512,160]{1,2,0:T(8,128)} copy(f32[2,512,160]{2,1,0:T(8,128)} %get-tuple-element.11) | data formatting | bytes 1310720 | tf_op jit(solution)/shard_map/update/pallas_call | solution.py:261
  162.7 0.0 copy-done.2
  162.7 1.1 copy.17
  163.8 0.0 copy-done.1
  163.8 1.1 copy.18
  (3 shorter events, 0.0 us)
Async XLA Ops:
  1.4 9.5 %collective-permute-start = (bf16[16,640]{1,0:T(8,128)(2,1)S(1)}, bf16[16,640]{1,0:T(8,128)(2,1)S(1)}, u32[]{:S(2)}, u32[]{:S(2)}) collective-permute-start(bf16[16,640]{1,0:T(8,128)(2,1)S(1)} %get-tuple-element.15), channel_id=1, source_target_pairs={{0,4},{4,8},{8,12},{12,16},{16,20},{20,24},{24,28},{28,32},{32,36}... | collective-permute-start | bytes 61448 | tf_op jit(solution)/shard_map/ppermute | solution.py:26
  6.3 5.1 %collective-permute-start.1 = (bf16[16,640]{1,0:T(8,128)(2,1)S(1)}, bf16[16,640]{1,0:T(8,128)(2,1)S(1)}, u32[]{:S(2)}, u32[]{:S(2)}) collective-permute-start(bf16[16,640]{1,0:T(8,128)(2,1)S(1)} %get-tuple-element.14), channel_id=1, source_target_pairs={{4,0},{8,4},{12,8},{16,12},{20,16},{24,20},{28,24},{32,28},{36,32}... | collective-permute-start | bytes 61448 | tf_op jit(solution)/shard_map/ppermute | solution.py:26
  9.0 5.1 %collective-permute-start.2 = (bf16[16,640]{1,0:T(8,128)(2,1)S(1)}, bf16[16,640]{1,0:T(8,128)(2,1)S(1)}, u32[]{:S(2)}, u32[]{:S(2)}) collective-permute-start(bf16[16,640]{1,0:T(8,128)(2,1)S(1)} %slice.11), channel_id=1, source_target_pairs={{4,0},{8,4},{12,8},{16,12},{20,16},{24,20},{28,24},{32,28},{36,32}... | collective-permute-start | bytes 61448 | tf_op jit(solution)/shard_map/ppermute | solution.py:26
  10.9 3.2 %copy-start.8 = (bf16[16,640]{1,0:T(8,128)(2,1)}, bf16[16,640]{1,0:T(8,128)(2,1)S(1)}, u32[]{:S(2)}) copy-start(bf16[16,640]{1,0:T(8,128)(2,1)S(1)} %collective-permute-done.refs_3_) | copy-start | bytes 61444
  11.4 2.7 %copy-start.9 = (bf16[16,640]{1,0:T(8,128)(2,1)}, bf16[16,640]{1,0:T(8,128)(2,1)S(1)}, u32[]{:S(2)}) copy-start(bf16[16,640]{1,0:T(8,128)(2,1)S(1)} %collective-permute-done.1.refs_4_) | copy-start | bytes 61444
  14.1 0.6 copy-start.10
  14.6 14.4 %copy-start.11 = (s32[2,1024,1]{1,2,0:T(1,128)S(1)}, s32[2,1024,1]{1,2,0:T(1,128)}, u32[]{:S(2)}) copy-start(s32[2,1024,1]{1,2,0:T(1,128)} %param.15) | copy-start | bytes 24580
  24.2 17.2 %collective-permute-start.3 = (bf16[320,1024]{1,0:T(8,128)(2,1)}, bf16[320,1024]{1,0:T(8,128)(2,1)S(1)}, u32[]{:S(2)}, u32[]{:S(2)}) collective-permute-start(bf16[320,1024]{1,0:T(8,128)(2,1)} %get-tuple-element.8), channel_id=1, source_target_pairs={{0,1},{1,2},{2,3},{3,0},{4,5},{5,6},{6,7},{7,4},{8,9},{9,10},{10,1... | collective-permute-start | bytes 1966088 | tf_op jit(solution)/shard_map/ppermute | solution.py:26
  25.4 30.2 %collective-permute-start.4 = (bf16[320,1024]{1,0:T(8,128)(2,1)}, bf16[320,1024]{1,0:T(8,128)(2,1)S(1)}, u32[]{:S(2)}, u32[]{:S(2)}) collective-permute-start(bf16[320,1024]{1,0:T(8,128)(2,1)} %get-tuple-element.9), channel_id=1, source_target_pairs={{0,2},{1,3},{2,0},{3,1},{4,6},{5,7},{6,4},{7,5},{8,10},{9,11},{10,... | collective-permute-start | bytes 1966088 | tf_op jit(solution)/shard_map/ppermute | solution.py:26
  27.9 27.7 %collective-permute-start.5 = (bf16[320,1024]{1,0:T(8,128)(2,1)}, bf16[320,1024]{1,0:T(8,128)(2,1)S(1)}, u32[]{:S(2)}, u32[]{:S(2)}) collective-permute-start(bf16[320,1024]{1,0:T(8,128)(2,1)} %get-tuple-element.10), channel_id=1, source_target_pairs={{0,3},{1,0},{2,1},{3,2},{4,7},{5,4},{6,5},{7,6},{8,11},{9,8},{10,9... | collective-permute-start | bytes 1966088 | tf_op jit(solution)/shard_map/ppermute | solution.py:26
  41.4 14.2 %copy-start.3 = (bf16[320,1024]{1,0:T(8,128)(2,1)}, bf16[320,1024]{1,0:T(8,128)(2,1)S(1)}, u32[]{:S(2)}) copy-start(bf16[320,1024]{1,0:T(8,128)(2,1)S(1)} %collective-permute-done.3.refs_3_) | copy-start | bytes 1966084
  55.6 0.8 copy-start.4
  55.6 1.0 copy-start.5
  69.6 13.1 %copy-start.6 = (f32[2,512,160]{1,2,0:T(8,128)S(1)}, f32[2,512,160]{1,2,0:T(8,128)}, u32[]{:S(2)}) copy-start(f32[2,512,160]{1,2,0:T(8,128)} %param.17) | copy-start | bytes 1966084
  69.6 78.2 %all-to-all-start = ((bf16[64,168,128]{2,1,0:T(8,128)(2,1)}), bf16[64,168,128]{2,1,0:T(8,128)(2,1)S(1)}, u32[]{:S(2)}, u32[]{:S(2)}) async-start(bf16[64,168,128]{2,1,0:T(8,128)(2,1)} %send.1), calls=%async_computation | async-start | bytes 5505024 | tf_op jit(solution)/shard_map/all_to_all | solution.py:297
  84.0 2.5 %copy-start.7 = (f32[2,512,160]{1,2,0:T(8,128)S(1)}, f32[2,512,160]{1,2,0:T(8,128)}, u32[]{:S(2)}) copy-start(f32[2,512,160]{1,2,0:T(8,128)} %param.19) | copy-start | bytes 1966084
  147.7 1.6 copy-start
  160.1 2.5 %copy-start.2 = (f32[2,512,160]{2,1,0:T(8,128)S(1)}, f32[2,512,160]{2,1,0:T(8,128)}, u32[]{:S(2)}) copy-start(f32[2,512,160]{2,1,0:T(8,128)} %get-tuple-element.12) | copy-start | bytes 1966084
  160.1 3.7 %copy-start.1 = (f32[2,512,160]{2,1,0:T(8,128)S(1)}, f32[2,512,160]{2,1,0:T(8,128)}, u32[]{:S(2)}) copy-start(f32[2,512,160]{2,1,0:T(8,128)} %get-tuple-element.13) | copy-start | bytes 1966084

commit v2 on v1

v2 whole, which is shorter than its diff:
```python
import jax
import jax.numpy as jnp
from jax import lax
from jax.experimental import pallas as pl
from jax.experimental.pallas import tpu as pltpu
from jax.sharding import PartitionSpec as P


beta_one = 0.9
beta_two = 0.95
learn_rate = 0.01
adam_steps = 10.0
epsilon = 1e-08

LANES = 128
HALF = 64
HALO = 16
DIGIT = 32
META = 8
SMALL = 32
WIDE = 64
ROWS_DIMS = (((1,), (1,)), ((), ()))
VMEM = pl.BlockSpec(memory_space=pltpu.VMEM)
SMEM = pl.BlockSpec(memory_space=pltpu.SMEM)
ANY = pl.BlockSpec(memory_space=pl.ANY)


def shift_by(block, axis, distance, wrap):
    size = lax.axis_size(axis)
    if wrap:
        route = [(i, (i + distance) % size) for i in range(size)]
    else:
        route = [(i, i + distance) for i in range(size) if 0 <= i + distance < size]
    return lax.ppermute(block, axis, route)


def whole(shape, dtype):
    return jax.ShapeDtypeStruct(shape, dtype)


def near(*arrays):
    return [pltpu.with_memory_space_constraint(x, pltpu.VMEM) for x in arrays]


def lane_below(rows, bound):
    return lax.broadcasted_iota(jnp.int32, (rows, LANES), 1) < bound


def ones_where(mask):
    return jnp.where(mask, 1.0, 0.0).astype(jnp.bfloat16)


def plan_kernel(owners_ref, row_ref, place_ref, start_ref, meta_ref, rank_ref, *, peers):
    heads, length = owners_ref.shape
    owner_of = lax.broadcasted_iota(jnp.int32, (peers, LANES), 0)
    before = lax.broadcasted_iota(jnp.int32, (LANES, 2 * LANES), 0)
    after = lax.broadcasted_iota(jnp.int32, (LANES, 2 * LANES), 1)
    counter = ones_where((before < after) | (after >= LANES))
    carry = jnp.zeros((heads * peers, LANES), jnp.float32)
    for block in range(length // LANES):
        lanes = slice(block * LANES, (block + 1) * LANES)
        named = [
            jnp.where(owners_ref[h : h + 1, lanes] == owner_of, 1.0, 0.0) for h in range(heads)
        ]
        named = jnp.concatenate(named, axis=0)
        counts = jnp.dot(
            named.astype(jnp.bfloat16), counter, preferred_element_type=jnp.float32
        )
        rank = named * (counts[:, :LANES] + carry)
        carry = carry + counts[:, LANES:]
        for h in range(heads):
            own = jnp.sum(rank[h * peers : (h + 1) * peers], axis=0, keepdims=True)
            rank_ref[h : h + 1, lanes] = own
    owner_wide = lax.broadcasted_iota(jnp.int32, (LANES, length), 0)
    column = lax.broadcasted_iota(jnp.int32, (LANES, length), 0)
    total = jnp.zeros((2 * peers, LANES), jnp.float32)
    for h in range(heads):
        owners = owners_ref[h : h + 1]
        below = ones_where(owners < owner_wide)
        starts = lax.dot_general(
            jnp.ones((8, length), jnp.bfloat16), below, ROWS_DIMS,
            preferred_element_type=jnp.float32,
        )
        start_ref[h : h + 1] = starts[0:1].astype(jnp.int32)
        named = jnp.where(owners == owner_wide[:peers], 1.0, 0.0)
        start = jnp.sum(below[:peers].astype(jnp.float32), axis=1, keepdims=True)
        first = jnp.sum(named * start, axis=0, keepdims=True)
        rank = rank_ref[h : h + 1]
        place_ref[h : h + 1] = (first + rank).astype(jnp.int32)
        number = row_ref[h : h + 1] + 1
        high = (number // DIGIT).astype(jnp.float32)
        low = (number % DIGIT).astype(jnp.float32)
        digits = jnp.concatenate([named * high, named * low], axis=0).astype(jnp.bfloat16)
        chosen = ones_where(rank.astype(jnp.int32) + h * HALF == column)
        total = total + lax.dot_general(
            digits, chosen, ROWS_DIMS, preferred_element_type=jnp.float32
        )
    meta_ref[...] = total


def plan(owners, rows, peers):
    heads, length = owners.shape
    return pl.pallas_call(
        lambda *refs: plan_kernel(*refs, peers=peers),
        out_shape=[
            whole((heads, length), jnp.int32),
            whole((heads, LANES), jnp.int32),
            whole((2 * peers, LANES), jnp.float32),
        ],
        scratch_shapes=[pltpu.VMEM((heads, length), jnp.float32)],
        name="plan",
    )(owners, rows)


def weight_copies(tab_ref, weight_ref, packed, sems, spans, tabs, heads, head_dim):
    copies = []
    place = 0
    for relative in range(tabs):
        base = ((tab_ref[0] + relative) % tabs) * (heads * head_dim)
        for low, count in spans:
            for h in range(heads):
                start = pl.multiple_of(base + (h * head_dim + low), 32)
                copies.append(
                    pltpu.make_async_copy(
                        weight_ref.at[pl.ds(start, count)],
                        packed.at[pl.ds(place, count)],
                        sems.at[len(copies)],
                    )
                )
                place += count
    return copies


def adjoint_kernel(
    tab_ref, cot_ref, value_ref, prior_ref, next_ref, gate_ref, taps_ref, weight_ref,
    scaled, own_ref, one_ref, two_ref, three_ref, value_pad, grad_pad, packed, sems,
    *, heads, head_dim, tabs
):
    copies = weight_copies(
        tab_ref, weight_ref, packed, sems, [(0, SMALL)], tabs, heads, head_dim
    )
    for copy in copies:
        copy.start()
    length, width = cot_ref.shape
    strips = width // LANES
    rows = LANES
    for strip in range(strips):
        lanes = slice(strip * LANES, (strip + 1) * LANES)
        value_pad[strip, :HALO] = prior_ref[:, lanes].astype(jnp.float32)
        value_pad[strip, HALO : HALO + length] = value_ref[:, lanes].astype(jnp.float32)
        value_pad[strip, HALO + length :] = next_ref[:HALO, lanes].astype(jnp.float32)

    def adjoint(strip, start, count, upstream):
        lanes = slice(strip * LANES, (strip + 1) * LANES)
        mixed = taps_ref[0:1, lanes] * value_pad[strip, pl.ds(start + HALO, count)]
        for tap in range(1, 4):
            mixed = mixed + taps_ref[tap : tap + 1, lanes] * value_pad[
                strip, pl.ds(start + HALO - 3 * tap, count)
            ]
        squashed = jax.nn.sigmoid(mixed)
        return upstream * squashed * (1.0 + mixed * (1.0 - squashed))

    def first(block, carry):
        start = pl.multiple_of(block * rows, rows)
        for strip in range(strips):
            lanes = slice(strip * LANES, (strip + 1) * LANES)
            upstream = cot_ref[pl.ds(start, rows), lanes].astype(jnp.float32)
            grad_pad[strip, pl.ds(start, rows)] = adjoint(strip, start, rows, upstream)
        return carry

    lax.fori_loop(0, length // rows, first, 0)
    for strip in range(strips):
        lanes = slice(strip * LANES, (strip + 1) * LANES)
        upstream = next_ref[HALO:, lanes].astype(jnp.float32)
        grad_pad[strip, length:] = adjoint(strip, length, HALO, upstream)

    def second(block, carry):
        start = pl.multiple_of(block * rows, rows)
        gate = jnp.broadcast_to(gate_ref[pl.ds(block, 1), :], (LANES, LANES)).T
        for strip in range(strips):
            lanes = slice(strip * LANES, (strip + 1) * LANES)
            total = cot_ref[pl.ds(start, rows), lanes].astype(jnp.float32)
            for tap in range(4):
                total = total + taps_ref[tap : tap + 1, lanes] * grad_pad[
                    strip, pl.ds(start + 3 * tap, rows)
                ]
            scaled[pl.ds(start, rows), lanes] = (gate * total).astype(jnp.bfloat16)
        return carry

    lax.fori_loop(0, length // rows, second, 0)
    for copy in copies:
        copy.wait()
    fold = length // 2
    left = lane_below(fold, HALF)
    halves = [
        lax.dot_general(
            scaled[part * fold : (part + 1) * fold], packed[...], ROWS_DIMS,
            preferred_element_type=jnp.float32,
        )
        for part in range(2)
    ]
    outs = [own_ref, one_ref, two_ref, three_ref]
    for tile in range(2):
        lanes = slice(tile * LANES, (tile + 1) * LANES)
        a, b = halves[0][:, lanes], halves[1][:, lanes]
        even = jnp.where(left, a, pltpu.roll(b, HALF, 1))
        odd = jnp.where(left, pltpu.roll(a, HALF, 1), b)
        outs[2 * tile][...] = even.astype(outs[2 * tile].dtype)
        outs[2 * tile + 1][...] = odd.astype(outs[2 * tile + 1].dtype)


def adjoint_terms(tab_index, cot, value, prior, following, gate, taps, weight, heads, head_dim, tabs):
    length, width = cot.shape
    strips = width // LANES
    folded = (length // 2, LANES)
    return pl.pallas_call(
        lambda *refs: adjoint_kernel(*refs, heads=heads, head_dim=head_dim, tabs=tabs),
        out_shape=[whole((length, width), jnp.bfloat16), whole(folded, jnp.float32)]
        + [whole(folded, jnp.bfloat16)] * (tabs - 1),
        in_specs=[SMEM] + [VMEM] * 6 + [ANY],
        out_specs=[VMEM] * (tabs + 1),
        scratch_shapes=[
            pltpu.VMEM((strips, length + 2 * HALO, LANES), jnp.float32),
            pltpu.VMEM((strips, length + HALO, LANES), jnp.float32),
            pltpu.VMEM((tabs * heads * SMALL, width), jnp.bfloat16),
            pltpu.SemaphoreType.DMA((tabs * heads,)),
        ],
        name="adjoint",
    )(tab_index, cot, value, prior, following, gate, taps, weight)


def project_kernel(
    tab_ref, scaled_ref, weight_ref, own_ref, one_ref, two_ref, three_ref, packed, sems,
    *, heads, head_dim, tabs
):
    spans = [(SMALL, WIDE), (SMALL + WIDE, WIDE)]
    copies = weight_copies(tab_ref, weight_ref, packed, sems, spans, tabs, heads, head_dim)
    for copy in copies:
        copy.start()
    for copy in copies:
        copy.wait()
    size = 2 * LANES
    for relative, out in enumerate([own_ref, one_ref, two_ref, three_ref]):
        term = lax.dot_general(
            scaled_ref[...], packed[relative * size : (relative + 1) * size], ROWS_DIMS,
            preferred_element_type=jnp.float32,
        )
        out[...] = term.astype(out.dtype)


def project(tab_index, scaled, weight, heads, head_dim, tabs):
    length, width = scaled.shape
    size = (length, 2 * LANES)
    return pl.pallas_call(
        lambda *refs: project_kernel(*refs, heads=heads, head_dim=head_dim, tabs=tabs),
        out_shape=[whole(size, jnp.float32)] + [whole(size, jnp.bfloat16)] * (tabs - 1),
        in_specs=[SMEM, VMEM, ANY],
        out_specs=[VMEM] * tabs,
        scratch_shapes=[
            pltpu.VMEM((tabs * 2 * LANES, width), jnp.bfloat16),
            pltpu.SemaphoreType.DMA((tabs * heads * 2,)),
        ],
        name="project",
    )(tab_index, scaled, weight)


def sort_tokens(place_ref, grads, ordered, tiles):
    heads, length = place_ref.shape
    rows = 256
    position = lax.broadcasted_iota(jnp.int32, (rows, length), 0)
    for h in range(heads):
        for tile in range(tiles):
            ordered[h, tile, length:] = jnp.zeros((HALF, LANES), jnp.float32)
        for step in range(length // rows):
            chosen = ones_where(place_ref[h : h + 1] - step * rows == position)
            got = jnp.dot(chosen, grads[...], preferred_element_type=jnp.float32)
            for tile in range(tiles):
                ordered[h, tile, step * rows : (step + 1) * rows] = got[
                    :, tile * LANES : (tile + 1) * LANES
                ]


def summed(refs, index):
    total = refs[0][index]
    for ref in refs[1:]:
        total = total + ref[index].astype(jnp.float32)
    return total


def send_small_kernel(
    start_ref, place_ref, meta_ref, own_ref, one_ref, two_ref, three_ref, out_ref, grads, ordered
):
    peers = out_ref.shape[0]
    fold = own_ref.shape[0]
    wide_left = lane_below(fold, HALF)
    total = summed([own_ref, one_ref, two_ref, three_ref], slice(None))
    turned = pltpu.roll(total, HALF, 1)
    grads[:fold] = jnp.where(wide_left, total, turned).astype(jnp.bfloat16)
    grads[fold:] = jnp.where(wide_left, turned, total).astype(jnp.bfloat16)
    sort_tokens(place_ref, grads, ordered, 1)
    lane = lax.broadcasted_iota(jnp.int32, (SMALL, LANES), 1)
    kind = lax.broadcasted_iota(jnp.int32, (META, LANES), 0)
    unroll = 4

    def body(step, carry):
        for part in range(unroll):
            peer = step * unroll + part
            pieces = []
            for half in range(2):
                for h in range(2):
                    start = start_ref[h, peer] + half * SMALL
                    pieces.append(ordered[h, 0, pl.ds(start, SMALL)])
            block = jnp.where(lane < 32, pieces[0], pieces[1])
            upper = jnp.where(lane < 96, pieces[2], pieces[3])
            block = jnp.where(lane < 64, block, upper)
            out_ref[peer, :SMALL] = block.astype(jnp.bfloat16)
            high = jnp.broadcast_to(meta_ref[pl.ds(peer, 1)], (META, LANES))
            low = jnp.broadcast_to(meta_ref[pl.ds(peers + peer, 1)], (META, LANES))
            digits = jnp.where(kind == 0, high, jnp.where(kind == 1, low, 0.0))
            out_ref[peer, SMALL:] = digits.astype(jnp.bfloat16)
        return carry

    lax.fori_loop(0, peers // unroll, body, 0)


def send_small(starts, places, meta, terms, peers):
    heads, length = places.shape
    return pl.pallas_call(
        send_small_kernel,
        out_shape=whole((peers, SMALL + META, LANES), jnp.bfloat16),
        in_specs=[SMEM] + [VMEM] * 6,
        out_specs=VMEM,
        scratch_shapes=[
            pltpu.VMEM((length, LANES), jnp.bfloat16),
            pltpu.VMEM((heads, 1, length + HALF, LANES), jnp.float32),
        ],
        name="send_small",
    )(starts, places, meta, terms[0], *near(*terms[1:]))


def send_wide_kernel(
    start_ref, place_ref, own_ref, one_ref, two_ref, three_ref, after_ref, out_ref, grads, ordered
):
    peers = out_ref.shape[0]
    grads[...] = summed([own_ref, one_ref, two_ref, three_ref], slice(None)).astype(jnp.bfloat16)
    sort_tokens(place_ref, grads, ordered, 2)
    left = lane_below(HALF, HALF)
    unroll = 2

    def body(step, carry):
        for part in range(unroll):
            peer = step * unroll + part
            for tile in range(2):
                a = ordered[0, tile, pl.ds(start_ref[0, peer], HALF)]
                b = ordered[1, tile, pl.ds(start_ref[1, peer], HALF)]
                out_ref[peer, tile * HALF : (tile + 1) * HALF] = jnp.where(left, a, b).astype(
                    jnp.bfloat16
                )
        return carry

    lax.fori_loop(0, peers // unroll, body, 0)


def send_wide(starts, places, terms, after, peers):
    heads, length = places.shape
    return pl.pallas_call(
        send_wide_kernel,
        out_shape=whole((peers, 2 * HALF, LANES), jnp.bfloat16),
        in_specs=[SMEM] + [VMEM] * 5 + [ANY],
        out_specs=VMEM,
        scratch_shapes=[
            pltpu.VMEM((length, 2 * LANES), jnp.bfloat16),
            pltpu.VMEM((heads, 2, length + HALF, LANES), jnp.float32),
        ],
        name="send_wide",
    )(starts, places, terms[0], *near(*terms[1:]), after)


def add_small_kernel(got_ref, grad_ref, hits_ref, number_ref, numbers):
    peers = got_ref.shape[0]
    heads, _, rows = grad_ref.shape
    for peer in range(peers):
        digits = got_ref[peer, SMALL:].astype(jnp.float32)
        numbers[peer : peer + 1] = digits[0:1] * float(DIGIT) + digits[1:2] - 1.0
    pairs = peers // 2
    even = numbers[pl.ds(0, pairs, stride=2)]
    odd = numbers[pl.ds(1, pairs, stride=2)]
    left = lane_below(pairs, HALF)
    number_ref[0] = jnp.where(left, even, pltpu.roll(odd, HALF, 1)).astype(jnp.int32)
    number_ref[1] = jnp.where(left, pltpu.roll(even, HALF, 1), odd).astype(jnp.int32)
    row_of = lax.broadcasted_iota(jnp.int32, (rows, LANES), 0)
    keep = lane_below(SMALL, HALF)
    totals = [jnp.zeros((rows, LANES), jnp.float32) for _ in range(heads)]
    group = 4
    for step in range(peers // group):
        parts = []
        for peer in range(step * group, (step + 1) * group):
            block = got_ref[peer, :SMALL].astype(jnp.float32)
            parts.append(jnp.where(keep, block, 1.0))
            parts.append(jnp.where(keep, pltpu.roll(block, HALF, 1), 1.0))
        block = jnp.concatenate(parts, axis=0).astype(jnp.bfloat16)
        for h in range(heads):
            chosen = [
                ones_where(number_ref[h, 2 * step + i : 2 * step + i + 1] == row_of)
                for i in range(group // 2)
            ]
            totals[h] = totals[h] + jnp.dot(
                jnp.concatenate(chosen, axis=1), block, preferred_element_type=jnp.float32
            )
    for h in range(heads):
        turned = totals[h].T
        grad_ref[h] = turned[h * SMALL : (h + 1) * SMALL]
        hits_ref[h] = turned[HALF : HALF + 8]


def add_small(got, heads, rows):
    peers = got.shape[0]
    return pl.pallas_call(
        add_small_kernel,
        out_shape=[
            whole((heads, SMALL, rows), jnp.float32),
            whole((heads, 8, rows), jnp.float32),
            whole((heads, peers // 2, LANES), jnp.int32),
        ],
        scratch_shapes=[pltpu.VMEM((peers, LANES), jnp.float32)],
        name="add_small",
    )(*near(got))


def update_kernel(
    got_ref, small_ref, hits_ref, number_ref, table_ref, one_ref, two_ref,
    new_table, new_one, new_two
):
    peers = got_ref.shape[0]
    heads, head_dim, rows = table_ref.shape
    row_of = lax.broadcasted_iota(jnp.int32, (rows, LANES), 0)
    totals = [jnp.zeros((rows, 2 * LANES), jnp.float32) for _ in range(heads)]
    group = 4
    for step in range(peers // group):
        members = range(step * group, (step + 1) * group)
        block = jnp.concatenate(
            [
                jnp.concatenate([got_ref[peer, :HALF] for peer in members], axis=0),
                jnp.concatenate([got_ref[peer, HALF:] for peer in members], axis=0),
            ],
            axis=1,
        )
        for h in range(heads):
            chosen = [
                ones_where(number_ref[h, 2 * step + i : 2 * step + i + 1] == row_of)
                for i in range(group // 2)
            ]
            totals[h] = totals[h] + jnp.dot(
                jnp.concatenate(chosen, axis=1), block, preferred_element_type=jnp.float32
            )
    left = lane_below(rows, HALF)
    turned = [
        jnp.where(
            left, totals[0][:, t * LANES : (t + 1) * LANES], totals[1][:, t * LANES : (t + 1) * LANES]
        ).T
        for t in range(2)
    ]
    for h in range(heads):
        own = slice(h * HALF, (h + 1) * HALF)
        grad = jnp.concatenate([small_ref[h], turned[0][own], turned[1][own]], axis=0)
        touched = jnp.broadcast_to(hits_ref[h, 0:1] > 0.5, (head_dim, rows))
        old_one, old_two, old_table = one_ref[h], two_ref[h], table_ref[h]
        first = beta_one * old_one + (1.0 - beta_one) * grad
        second = beta_two * old_two + (1.0 - beta_two) * grad * grad
        update = (first / (1.0 - beta_one**adam_steps)) / (
            jnp.sqrt(second / (1.0 - beta_two**adam_steps)) + epsilon
        )
        new_table[h] = jnp.where(touched, old_table - learn_rate * update, old_table)
        new_one[h] = jnp.where(touched, first, old_one)
        new_two[h] = jnp.where(touched, second, old_two)


def updated(got, small, hits, numbers, table, one, two):
    return pl.pallas_call(
        update_kernel,
        out_shape=[whole(table.shape, jnp.float32)] * 3,
        name="update",
    )(*near(got), small, hits, numbers, table, one, two)


def shards(
    cotangent,
    saved_value,
    gate_scale,
    conv_weight,
    value_weight,
    owner_ids,
    local_row,
    row_table,
    moment_one,
    moment_two,
):
    length = cotangent.shape[0]
    heads, rows, head_dim = row_table.shape
    peers = lax.axis_size("seq")
    tabs = lax.axis_size("tab")
    tab_index = lax.axis_index("tab").astype(jnp.int32).reshape(1)
    prior = shift_by(saved_value[length - HALO :], "seq", 1, False)
    following = jnp.concatenate([saved_value[:HALO], cotangent[:HALO]], axis=0)
    following = shift_by(following, "seq", -1, False)
    places, starts, meta = plan(owner_ids[:, :, 0], local_row, peers)
    scaled, *small = adjoint_terms(
        tab_index, cotangent, saved_value, prior, following, gate_scale.reshape(-1, LANES),
        conv_weight, value_weight, heads, head_dim, tabs,
    )
    wide = list(project(tab_index, scaled, value_weight, heads, head_dim, tabs))
    for i in range(1, tabs):
        small[i] = shift_by(small[i], "tab", i, True)
        wide[i] = shift_by(wide[i], "tab", i, True)
    blocks = send_small(starts, places, meta, small, peers)
    got = lax.all_to_all(blocks, "seq", split_axis=0, concat_axis=0, tiled=True)
    wide_blocks = send_wide(starts, places, wide, blocks, peers)
    wide_got = lax.all_to_all(wide_blocks, "seq", split_axis=0, concat_axis=0, tiled=True)
    small_grad, hits, numbers = add_small(got, heads, rows)
    state = [jnp.swapaxes(x, 1, 2) for x in (row_table, moment_one, moment_two)]
    new = updated(wide_got, small_grad, hits, numbers, *state)
    return tuple(jnp.swapaxes(x, 1, 2) for x in new)


def solution(mesh):
    in_specs = (
        P("seq", "tab"),
        P("seq", "tab"),
        P("seq"),
        P(None, "tab"),
        P(None, "tab"),
        P("tab", "seq", None),
        P("tab", "seq"),
        P("tab", "seq", None),
        P("tab", "seq", None),
        P("tab", "seq", None),
    )
    out_specs = (P("tab", "seq", None), P("tab", "seq", None), P("tab", "seq", None))
    return jax.shard_map(shards, mesh=mesh, in_specs=in_specs, out_specs=out_specs, check_vma=False)
```

time: 165 us -> 149 us (0.903)
  waiting for transfers between devices: 87.4 us -> 73.5 us
  starting transfers between devices: 26.7 us -> 40.4 us
  local copies, waits for them, and re-layouts: 15.2 us -> 2.71 us
  Pallas kernels: 35 us -> 30.8 us
    all_to_all x1, waiting for transfers between devices: 59.9 us -> 0.01 us  [shards(): got = lax.all_to_all(blocks, 'seq', split_axis=0, concat_axis=0, tiled=True)]
    all_to_all x0 -> x1, waiting for transfers between devices: none -> 48 us  [shards(): lax.all_to_all(wide_blocks, 'seq', split_axis=0, concat_axis=0, tiled=True)]
    all_to_all x0 -> x1, starting transfers between devices: none -> 11.3 us  [shards(): lax.all_to_all(wide_blocks, 'seq', split_axis=0, concat_axis=0, tiled=True)]
    unnamed x28 -> x7, local copies, waits for them, and re-layouts: 8.94 us -> 1.23 us
    pallas_call x1, Pallas kernels: 10.9 us -> 5.58 us  [updated(): pl.pallas_call(update_kernel, out_shape=[whole(table.shape, jnp.float32)]...]
    pallas_call x3 -> x0, local copies, waits for them, and re-layouts: 4.81 us -> none  [updated(): pl.pallas_call(update_kernel, out_shape=[whole(table.shape, jnp.float32)]...]
    ppermute x6 -> x8, starting transfers between devices: 13.6 us -> 16 us  [shift_by(): return lax.ppermute(block, axis, route)]
    ppermute x6 -> x8, waiting for transfers between devices: 27.5 us -> 25.4 us  [shift_by(): return lax.ppermute(block, axis, route)]
  transfers between devices with their start and end apart: 7 -> 10, of which waited for: 5 -> 5; matrix products, arithmetic and copies ran while one was open for 4% -> 0% of each run, Pallas kernels for 1% -> 10%
where the time goes in v2:
time: 149 us; the launch traced here: 148 us
  waiting for transfers between devices  73.5 us (49%)
  starting transfers between devices  40.4 us (27%)
  Pallas kernels  30.8 us (21%)
  local copies, waits for them, and re-layouts  2.71 us (2%)
    all_to_all x1, waiting for transfers between devices, shards(): lax.all_to_all(wide_blocks, 'seq', split_axis=0, concat_axis=0, tiled=True)  48 us
    ppermute x8, waiting for transfers between devices, shift_by(): return lax.ppermute(block, axis, route)  25.4 us
    ppermute x8, starting transfers between devices, shift_by(): return lax.ppermute(block, axis, route)  16 us
    all_to_all x1, starting transfers between devices, shards(): got = lax.all_to_all(blocks, 'seq', split_axis=0, concat_axis=0, tiled=True)  13.2 us
    all_to_all x1, starting transfers between devices, shards(): lax.all_to_all(wide_blocks, 'seq', split_axis=0, concat_axis=0, tiled=True)  11.3 us
    pallas_call x1, Pallas kernels, adjoint_terms(): pl.pallas_call(lambda *refs: adjoint_kernel(*refs, heads=heads, head_dim=...  6.12 us
    pallas_call x1, Pallas kernels, project(): pl.pallas_call(lambda *refs: project_kernel(*refs, heads=heads, head_dim=...  5.6 us
    pallas_call x1, Pallas kernels, updated(): pl.pallas_call(update_kernel, out_shape=[whole(table.shape, jnp.float32)]...  5.58 us
  transfers between devices with their start and end apart: 10, of which 5 were waited for; matrix products, arithmetic and copies ran while one was open for 0% of the time, Pallas kernels for 10%

profile of v2, /device:TPU:1, one launch (start us, length us, event | category | flops | bytes accessed | tf_op | source)
XLA Modules:
  0.0 148.1 jit_solution(7609486637972578787)
XLA Ops:
  0.6 0.8 fusion
  1.4 0.7 slice.11
  2.1 5.1 %collective-permute-start.1 = (bf16[32,640]{1,0:T(8,128)(2,1)S(1)}, bf16[32,640]{1,0:T(8,128)(2,1)S(1)}, u32[]{:S(2)}, u32[]{:S(2)}) collective-permute-start(bf16[32,640]{1,0:T(8,128)(2,1)S(1)} %pad_maximum_fusion), channel_id=1, source_target_pairs={{4,0},{8,4},{12,8},{16,12},{20,16},{24,20},{28,24},{32,28},{36,32}... | collective-permute-start | bytes 122888 | tf_op jit(solution)/shard_map/ppermute | solution.py:34
  7.2 1.9 %collective-permute-start = (bf16[16,640]{1,0:T(8,128)(2,1)S(1)}, bf16[16,640]{1,0:T(8,128)(2,1)S(1)}, u32[]{:S(2)}, u32[]{:S(2)}) collective-permute-start(bf16[16,640]{1,0:T(8,128)(2,1)S(1)} %get-tuple-element.40), channel_id=1, source_target_pairs={{0,4},{4,8},{8,12},{12,16},{16,20},{20,24},{24,28},{28,32},{32,36}... | collective-permute-start | bytes 61448 | tf_op jit(solution)/shard_map/ppermute | solution.py:34
  9.2 1.2 collective-permute-done.refs_3_
  10.3 0.0 copy-start.1
  10.3 0.0 collective-permute-done.1.refs_4_
  10.3 0.0 copy-start
  10.3 0.6 copy-done.1
  10.9 0.0 copy-done
  10.9 0.0 copy-start.2
  10.9 6.1 %adjoint.1 = (bf16[1024,640]{1,0:T(8,128)(2,1)}, f32[512,128]{1,0:T(8,128)}, bf16[512,128]{1,0:T(8,128)(2,1)}, bf16[512,128]{1,0:T(8,128)(2,1)}, bf16[512,128]{1,0:T(8,128)(2,1)}) custom-call(s32[1]{0:T(128)} %bitcast.refs_0_, bf16[1024,640]{1,0:T(8,128)(2,1)} %refs_1_.3, bf16[1024,640]{1,0:T(8,128)(2,1)} %refs_2_.2, bf16[16,640]{1,0:T(8,128)(2,1)} %copy-done.1, ...), custom_call_target="tpu_custom_call" | custom-call | tf_op jit(solution)/shard_map/adjoint/pallas_call | solution.py:216
  17.1 0.8 collective-permute-start.5
  17.9 2.5 %collective-permute-start.6 = (bf16[512,128]{1,0:T(8,128)(2,1)}, bf16[512,128]{1,0:T(8,128)(2,1)S(1)}, u32[]{:S(2)}, u32[]{:S(2)}) collective-permute-start(bf16[512,128]{1,0:T(8,128)(2,1)} %get-tuple-element.31), channel_id=1, source_target_pairs={{0,2},{1,3},{2,0},{3,1},{4,6},{5,7},{6,4},{7,5},{8,10},{9,11},{10,... | collective-permute-start | bytes 393224 | tf_op jit(solution)/shard_map/ppermute | solution.py:34
  20.3 1.1 collective-permute-start.7
  21.5 0.0 copy-done.2
  21.5 0.6 copy.15
  22.1 2.3 %plan.1 = (s32[2,1024]{1,0:T(2,128)}, s32[2,128]{1,0:T(2,128)}, f32[128,128]{1,0:T(8,128)}) custom-call(s32[2,1024]{1,0:T(2,128)} %bitcast.14, s32[2,1024]{1,0:T(2,128)} %refs_1_.2), custom_call_target="tpu_custom_call" | custom-call | tf_op jit(solution)/shard_map/plan/pallas_call | solution.py:103
  24.4 0.0 collective-permute-done.5.one_ref
  24.4 2.2 %collective-permute-done.6.two_ref = bf16[512,128]{1,0:T(8,128)(2,1)S(1)} collective-permute-done((bf16[512,128]{1,0:T(8,128)(2,1)}, bf16[512,128]{1,0:T(8,128)(2,1)S(1)}, u32[]{:S(2)}, u32[]{:S(2)}) %collective-permute-start.6) | collective-permute-done | bytes 131104 | tf_op jit(solution)/shard_map/ppermute | solution.py:34
  26.6 0.0 collective-permute-done.7.three_ref
  26.6 3.6 %send_small.1.after_ref = bf16[64,40,128]{2,1,0:T(8,128)(2,1)} custom-call(s32[2,128]{1,0:T(2,128)} %get-tuple-element.21.start_ref, s32[2,1024]{1,0:T(2,128)} %get-tuple-element.22.place_ref, f32[128,128]{1,0:T(8,128)} %get-tuple-element.28.meta_ref, f32[512,128]{1,0:T(8,128)} %get-tuple-element.29.own_ref, ...), custom_call_target="tpu_custom_call" | custom-call | tf_op jit(solution)/shard_map/send_small/pallas_call | solution.py:328
  30.2 13.2 %all-to-all-start.1 = ((bf16[64,40,128]{2,1,0:T(8,128)(2,1)}), bf16[64,40,128]{2,1,0:T(8,128)(2,1)S(1)}, u32[]{:S(2)}, u32[]{:S(2)}) async-start(bf16[64,40,128]{2,1,0:T(8,128)(2,1)} %send_small.1.after_ref), calls=%async_computation.1 | async-start | bytes 1310720 | tf_op jit(solution)/shard_map/all_to_all | solution.py:516
  43.4 5.6 %project.1 = (f32[1024,256]{1,0:T(8,128)}, bf16[1024,256]{1,0:T(8,128)(2,1)}, bf16[1024,256]{1,0:T(8,128)(2,1)}, bf16[1024,256]{1,0:T(8,128)(2,1)}) custom-call(s32[1]{0:T(128)} %bitcast.refs_0_, bf16[1024,640]{1,0:T(8,128)(2,1)} %get-tuple-element.23.refs_1_, bf16[1280,640]{1,0:T(8,128)(2,1)} %refs_2_.3), custom_call_target="tpu_custom_call" | custom-call | tf_op jit(solution)/shard_map/project/pallas_call | solution.py:254
  49.0 1.1 collective-permute-start.2
  50.1 2.4 %collective-permute-start.3 = (bf16[1024,256]{1,0:T(8,128)(2,1)}, bf16[1024,256]{1,0:T(8,128)(2,1)S(1)}, u32[]{:S(2)}, u32[]{:S(2)}) collective-permute-start(bf16[1024,256]{1,0:T(8,128)(2,1)} %get-tuple-element.26), channel_id=1, source_target_pairs={{0,2},{1,3},{2,0},{3,1},{4,6},{5,7},{6,4},{7,5},{8,10},{9,11},{10,... | collective-permute-start | bytes 1572872 | tf_op jit(solution)/shard_map/ppermute | solution.py:34
  52.6 1.0 collective-permute-start.4
  53.5 10.0 %collective-permute-done.2.one_ref = bf16[1024,256]{1,0:T(8,128)(2,1)S(1)} collective-permute-done((bf16[1024,256]{1,0:T(8,128)(2,1)}, bf16[1024,256]{1,0:T(8,128)(2,1)S(1)}, u32[]{:S(2)}, u32[]{:S(2)}) %collective-permute-start.2) | collective-permute-done | bytes 524320 | tf_op jit(solution)/shard_map/ppermute | solution.py:34
  63.5 12.0 %collective-permute-done.3.two_ref = bf16[1024,256]{1,0:T(8,128)(2,1)S(1)} collective-permute-done((bf16[1024,256]{1,0:T(8,128)(2,1)}, bf16[1024,256]{1,0:T(8,128)(2,1)S(1)}, u32[]{:S(2)}, u32[]{:S(2)}) %collective-permute-start.3) | collective-permute-done | bytes 524320 | tf_op jit(solution)/shard_map/ppermute | solution.py:34
  75.6 0.0 collective-permute-done.4.three_ref
  75.6 4.5 %send_wide.1 = bf16[64,128,128]{2,1,0:T(8,128)(2,1)} custom-call(s32[2,128]{1,0:T(2,128)} %get-tuple-element.21.start_ref, s32[2,1024]{1,0:T(2,128)} %get-tuple-element.22.place_ref, f32[1024,256]{1,0:T(8,128)} %get-tuple-element.24.own_ref, bf16[1024,256]{1,0:T(8,128)(2,1)S(1)} %collective-permute-done.2.one_ref, ...), custom_call_target="tpu_custom_call" | custom-call | tf_op jit(solution)/shard_map/send_wide/pallas_call | solution.py:366
  80.1 0.0 all-to-all-done.1.got_ref
  80.1 11.3 %all-to-all-start = ((bf16[64,128,128]{2,1,0:T(8,128)(2,1)}), bf16[64,128,128]{2,1,0:T(8,128)(2,1)S(1)}, u32[]{:S(2)}, u32[]{:S(2)}) async-start(bf16[64,128,128]{2,1,0:T(8,128)(2,1)} %send_wide.1), calls=%async_computation | async-start | bytes 4194304 | tf_op jit(solution)/shard_map/all_to_all | solution.py:518
  91.3 3.2 %add_small.1 = (f32[2,32,512]{2,1,0:T(8,128)}, f32[2,8,512]{2,1,0:T(8,128)}, s32[2,32,128]{2,1,0:T(8,128)}) custom-call(bf16[64,40,128]{2,1,0:T(8,128)(2,1)S(1)} %all-to-all-done.1.got_ref), custom_call_target="tpu_custom_call" | custom-call | tf_op jit(solution)/shard_map/add_small/pallas_call | solution.py:418
  94.5 48.0 %all-to-all-done.got_ref = bf16[64,128,128]{2,1,0:T(8,128)(2,1)S(1)} async-done(((bf16[64,128,128]{2,1,0:T(8,128)(2,1)}), bf16[64,128,128]{2,1,0:T(8,128)(2,1)S(1)}, u32[]{:S(2)}, u32[]{:S(2)}) %all-to-all-start) | async-done | bytes 2097184 | tf_op jit(solution)/shard_map/all_to_all | solution.py:518
  142.5 5.6 %update.1 = (f32[2,160,512]{2,1,0:T(8,128)}, f32[2,160,512]{2,1,0:T(8,128)}, f32[2,160,512]{2,1,0:T(8,128)}) custom-call(bf16[64,128,128]{2,1,0:T(8,128)(2,1)S(1)} %all-to-all-done.got_ref, f32[2,32,512]{2,1,0:T(8,128)} %get-tuple-element.33.small_ref, f32[2,8,512]{2,1,0:T(8,128)} %get-tuple-element.34.hits_ref, s32[2,32,128]{2,1,0:T(8,128)} %get-tuple-element.35.number_ref, ...), custom_call_target="tpu_custom_call" | custom-call | tf_op jit(solution)/shard_map/update/pallas_call | solution.py:479
  (1 shorter events, 0.0 us)
Async XLA Ops:
  2.1 8.2 %collective-permute-start.1 = (bf16[32,640]{1,0:T(8,128)(2,1)S(1)}, bf16[32,640]{1,0:T(8,128)(2,1)S(1)}, u32[]{:S(2)}, u32[]{:S(2)}) collective-permute-start(bf16[32,640]{1,0:T(8,128)(2,1)S(1)} %pad_maximum_fusion), channel_id=1, source_target_pairs={{4,0},{8,4},{12,8},{16,12},{20,16},{24,20},{28,24},{32,28},{36,32}... | collective-permute-start | bytes 122888 | tf_op jit(solution)/shard_map/ppermute | solution.py:34
  7.2 3.1 %collective-permute-start = (bf16[16,640]{1,0:T(8,128)(2,1)S(1)}, bf16[16,640]{1,0:T(8,128)(2,1)S(1)}, u32[]{:S(2)}, u32[]{:S(2)}) collective-permute-start(bf16[16,640]{1,0:T(8,128)(2,1)S(1)} %get-tuple-element.40), channel_id=1, source_target_pairs={{0,4},{4,8},{8,12},{12,16},{16,20},{20,24},{24,28},{28,32},{32,36}... | collective-permute-start | bytes 61448 | tf_op jit(solution)/shard_map/ppermute | solution.py:34
  10.3 0.6 copy-start.1
  10.3 0.6 copy-start
  10.9 10.6 %copy-start.2 = (s32[2,1024,1]{1,2,0:T(1,128)S(1)}, s32[2,1024,1]{1,2,0:T(1,128)}, u32[]{:S(2)}) copy-start(s32[2,1024,1]{1,2,0:T(1,128)} %param.15) | copy-start | bytes 24580
  17.1 7.3 %collective-permute-start.5 = (bf16[512,128]{1,0:T(8,128)(2,1)}, bf16[512,128]{1,0:T(8,128)(2,1)S(1)}, u32[]{:S(2)}, u32[]{:S(2)}) collective-permute-start(bf16[512,128]{1,0:T(8,128)(2,1)} %get-tuple-element.30), channel_id=1, source_target_pairs={{0,1},{1,2},{2,3},{3,0},{4,5},{5,6},{6,7},{7,4},{8,9},{9,10},{10,1... | collective-permute-start | bytes 393224 | tf_op jit(solution)/shard_map/ppermute | solution.py:34
  17.9 8.7 %collective-permute-start.6 = (bf16[512,128]{1,0:T(8,128)(2,1)}, bf16[512,128]{1,0:T(8,128)(2,1)S(1)}, u32[]{:S(2)}, u32[]{:S(2)}) collective-permute-start(bf16[512,128]{1,0:T(8,128)(2,1)} %get-tuple-element.31), channel_id=1, source_target_pairs={{0,2},{1,3},{2,0},{3,1},{4,6},{5,7},{6,4},{7,5},{8,10},{9,11},{10,... | collective-permute-start | bytes 393224 | tf_op jit(solution)/shard_map/ppermute | solution.py:34
  20.3 6.2 %collective-permute-start.7 = (bf16[512,128]{1,0:T(8,128)(2,1)}, bf16[512,128]{1,0:T(8,128)(2,1)S(1)}, u32[]{:S(2)}, u32[]{:S(2)}) collective-permute-start(bf16[512,128]{1,0:T(8,128)(2,1)} %get-tuple-element.32), channel_id=1, source_target_pairs={{0,3},{1,0},{2,1},{3,2},{4,7},{5,4},{6,5},{7,6},{8,11},{9,8},{10,9... | collective-permute-start | bytes 393224 | tf_op jit(solution)/shard_map/ppermute | solution.py:34
  30.2 49.9 %all-to-all-start.1 = ((bf16[64,40,128]{2,1,0:T(8,128)(2,1)}), bf16[64,40,128]{2,1,0:T(8,128)(2,1)S(1)}, u32[]{:S(2)}, u32[]{:S(2)}) async-start(bf16[64,40,128]{2,1,0:T(8,128)(2,1)} %send_small.1.after_ref), calls=%async_computation.1 | async-start | bytes 1310720 | tf_op jit(solution)/shard_map/all_to_all | solution.py:516
  49.0 14.5 %collective-permute-start.2 = (bf16[1024,256]{1,0:T(8,128)(2,1)}, bf16[1024,256]{1,0:T(8,128)(2,1)S(1)}, u32[]{:S(2)}, u32[]{:S(2)}) collective-permute-start(bf16[1024,256]{1,0:T(8,128)(2,1)} %get-tuple-element.25), channel_id=1, source_target_pairs={{0,1},{1,2},{2,3},{3,0},{4,5},{5,6},{6,7},{7,4},{8,9},{9,10},{10,1... | collective-permute-start | bytes 1572872 | tf_op jit(solution)/shard_map/ppermute | solution.py:34
  50.1 25.4 %collective-permute-start.3 = (bf16[1024,256]{1,0:T(8,128)(2,1)}, bf16[1024,256]{1,0:T(8,128)(2,1)S(1)}, u32[]{:S(2)}, u32[]{:S(2)}) collective-permute-start(bf16[1024,256]{1,0:T(8,128)(2,1)} %get-tuple-element.26), channel_id=1, source_target_pairs={{0,2},{1,3},{2,0},{3,1},{4,6},{5,7},{6,4},{7,5},{8,10},{9,11},{10,... | collective-permute-start | bytes 1572872 | tf_op jit(solution)/shard_map/ppermute | solution.py:34
  52.6 23.0 %collective-permute-start.4 = (bf16[1024,256]{1,0:T(8,128)(2,1)}, bf16[1024,256]{1,0:T(8,128)(2,1)S(1)}, u32[]{:S(2)}, u32[]{:S(2)}) collective-permute-start(bf16[1024,256]{1,0:T(8,128)(2,1)} %get-tuple-element.27), channel_id=1, source_target_pairs={{0,3},{1,0},{2,1},{3,2},{4,7},{5,4},{6,5},{7,6},{8,11},{9,8},{10,9... | collective-permute-start | bytes 1572872 | tf_op jit(solution)/shard_map/ppermute | solution.py:34
  80.1 62.5 %all-to-all-start = ((bf16[64,128,128]{2,1,0:T(8,128)(2,1)}), bf16[64,128,128]{2,1,0:T(8,128)(2,1)S(1)}, u32[]{:S(2)}, u32[]{:S(2)}) async-start(bf16[64,128,128]{2,1,0:T(8,128)(2,1)} %send_wide.1), calls=%async_computation | async-start | bytes 4194304 | tf_op jit(solution)/shard_map/all_to_all | solution.py:518

commit v3 on v2

--- a/solution.py
+++ b/solution.py
@@ -17,12 +17,14 @@
 HALO = 16
 DIGIT = 32
 META = 8
+PIECES = 4
 SMALL = 32
 WIDE = 64
 ROWS_DIMS = (((1,), (1,)), ((), ()))
 VMEM = pl.BlockSpec(memory_space=pltpu.VMEM)
 SMEM = pl.BlockSpec(memory_space=pltpu.SMEM)
 ANY = pl.BlockSpec(memory_space=pl.ANY)
+LIMIT = pltpu.CompilerParams(vmem_limit_bytes=24 << 20)
 
 
 def shift_by(block, axis, distance, wrap):
@@ -38,10 +40,18 @@
     return jax.ShapeDtypeStruct(shape, dtype)
 
 
+def kept(shape, dtype):
+    return pltpu.VMEM(shape, dtype)
+
+
 def near(*arrays):
     return [pltpu.with_memory_space_constraint(x, pltpu.VMEM) for x in arrays]
 
 
+def far(*arrays):
+    return [pltpu.with_memory_space_constraint(x, pltpu.HBM) for x in arrays]
+
+
 def lane_below(rows, bound):
     return lax.broadcasted_iota(jnp.int32, (rows, LANES), 1) < bound
 
@@ -51,7 +61,7 @@
 
 
 def plan_kernel(owners_ref, row_ref, place_ref, start_ref, meta_ref, rank_ref, *, peers):
-    heads, length = owners_ref.shape
+    heads, _, length = owners_ref.shape
     owner_of = lax.broadcasted_iota(jnp.int32, (peers, LANES), 0)
     before = lax.broadcasted_iota(jnp.int32, (LANES, 2 * LANES), 0)
     after = lax.broadcasted_iota(jnp.int32, (LANES, 2 * LANES), 1)
@@ -60,7 +70,7 @@
     for block in range(length // LANES):
         lanes = slice(block * LANES, (block + 1) * LANES)
         named = [
-            jnp.where(owners_ref[h : h + 1, lanes] == owner_of, 1.0, 0.0) for h in range(heads)
+            jnp.where(owners_ref[h, :, lanes] == owner_of, 1.0, 0.0) for h in range(heads)
         ]
         named = jnp.concatenate(named, axis=0)
         counts = jnp.dot(
@@ -75,7 +85,7 @@
     column = lax.broadcasted_iota(jnp.int32, (LANES, length), 0)
     total = jnp.zeros((2 * peers, LANES), jnp.float32)
     for h in range(heads):
-        owners = owners_ref[h : h + 1]
+        owners = owners_ref[h]
         below = ones_where(owners < owner_wide)
         starts = lax.dot_general(
             jnp.ones((8, length), jnp.bfloat16), below, ROWS_DIMS,
@@ -99,7 +109,7 @@
 
 
 def plan(owners, rows, peers):
-    heads, length = owners.shape
+    heads, _, length = owners.shape
     return pl.pallas_call(
         lambda *refs: plan_kernel(*refs, peers=peers),
         out_shape=[
@@ -108,14 +118,17 @@
             whole((2 * peers, LANES), jnp.float32),
         ],
         scratch_shapes=[pltpu.VMEM((heads, length), jnp.float32)],
+        compiler_params=LIMIT,
         name="plan",
-    )(owners, rows)
-
-
-def weight_copies(tab_ref, weight_ref, packed, sems, spans, tabs, heads, head_dim):
+    )(*far(owners, rows))
+
+
+def weight_copies(
+    tab_ref, weight_ref, packed, sems, spans, tabs, heads, head_dim, relatives=None
+):
     copies = []
     place = 0
-    for relative in range(tabs):
+    for relative in range(tabs) if relatives is None else relatives:
         base = ((tab_ref[0] + relative) % tabs) * (heads * head_dim)
         for low, count in spans:
             for h in range(heads):
@@ -132,22 +145,31 @@
 
 
 def adjoint_kernel(
-    tab_ref, cot_ref, value_ref, prior_ref, next_ref, gate_ref, taps_ref, weight_ref,
-    scaled, own_ref, one_ref, two_ref, three_ref, value_pad, grad_pad, packed, sems,
+    tab_ref, cot_far, value_far, prior_ref, next_ref, gate_ref, taps_ref, weight_ref, after_ref,
+    scaled, own_ref, one_ref, two_ref, three_ref,
+    cot_ref, value_ref, value_pad, grad_pad, packed, sems, cot_sems, value_sems,
     *, heads, head_dim, tabs
 ):
+    length, width = cot_ref.shape
+    piece = length // PIECES
+    loads = []
+    for index in range(PIECES):
+        part = pl.ds(index * piece, piece)
+        for source, target, own in (
+            (value_far, value_ref, value_sems), (cot_far, cot_ref, cot_sems)
+        ):
+            loads.append(pltpu.make_async_copy(source.at[part], target.at[part], own.at[index]))
+            loads[-1].start()
     copies = weight_copies(
         tab_ref, weight_ref, packed, sems, [(0, SMALL)], tabs, heads, head_dim
     )
     for copy in copies:
         copy.start()
-    length, width = cot_ref.shape
     strips = width // LANES
     rows = LANES
     for strip in range(strips):
         lanes = slice(strip * LANES, (strip + 1) * LANES)
         value_pad[strip, :HALO] = prior_ref[:, lanes].astype(jnp.float32)
-        value_pad[strip, HALO : HALO + length] = value_ref[:, lanes].astype(jnp.float32)
         value_pad[strip, HALO + length :] = next_ref[:HALO, lanes].astype(jnp.float32)
 
     def adjoint(strip, start, count, upstream):
@@ -164,11 +186,17 @@
         start = pl.multiple_of(block * rows, rows)
         for strip in range(strips):
             lanes = slice(strip * LANES, (strip + 1) * LANES)
+            value_pad[strip, pl.ds(start + HALO, rows)] = value_ref[
+                pl.ds(start, rows), lanes
+            ].astype(jnp.float32)
             upstream = cot_ref[pl.ds(start, rows), lanes].astype(jnp.float32)
             grad_pad[strip, pl.ds(start, rows)] = adjoint(strip, start, rows, upstream)
         return carry
 
-    lax.fori_loop(0, length // rows, first, 0)
+    for index in range(PIECES):
+        loads[2 * index].wait()
+        loads[2 * index + 1].wait()
+        lax.fori_loop(index * (piece // rows), (index + 1) * (piece // rows), first, 0)
     for strip in range(strips):
         lanes = slice(strip * LANES, (strip + 1) * LANES)
         upstream = next_ref[HALO:, lanes].astype(jnp.float32)
@@ -209,59 +237,73 @@
         outs[2 * tile + 1][...] = odd.astype(outs[2 * tile + 1].dtype)
 
 
-def adjoint_terms(tab_index, cot, value, prior, following, gate, taps, weight, heads, head_dim, tabs):
+def adjoint_terms(
+    tab_index, cot, value, prior, following, gate, taps, weight, after, heads, head_dim, tabs
+):
     length, width = cot.shape
     strips = width // LANES
     folded = (length // 2, LANES)
     return pl.pallas_call(
         lambda *refs: adjoint_kernel(*refs, heads=heads, head_dim=head_dim, tabs=tabs),
-        out_shape=[whole((length, width), jnp.bfloat16), whole(folded, jnp.float32)]
-        + [whole(folded, jnp.bfloat16)] * (tabs - 1),
-        in_specs=[SMEM] + [VMEM] * 6 + [ANY],
+        out_shape=[kept((length, width), jnp.bfloat16), kept(folded, jnp.float32)]
+        + [kept(folded, jnp.bfloat16)] * (tabs - 1),
+        in_specs=[SMEM] + [ANY] * 2 + [VMEM] * 4 + [ANY] * 2,
         out_specs=[VMEM] * (tabs + 1),
         scratch_shapes=[
+            pltpu.VMEM((length, width), jnp.bfloat16),
+            pltpu.VMEM((length, width), jnp.bfloat16),
             pltpu.VMEM((strips, length + 2 * HALO, LANES), jnp.float32),
             pltpu.VMEM((strips, length + HALO, LANES), jnp.float32),
             pltpu.VMEM((tabs * heads * SMALL, width), jnp.bfloat16),
             pltpu.SemaphoreType.DMA((tabs * heads,)),
+            pltpu.SemaphoreType.DMA((PIECES,)),
+            pltpu.SemaphoreType.DMA((PIECES,)),
         ],
+        compiler_params=LIMIT,
         name="adjoint",
-    )(tab_index, cot, value, prior, following, gate, taps, weight)
+    )(tab_index, *far(cot, value), *near(prior, following), *far(gate, taps, weight), after)
 
 
 def project_kernel(
-    tab_ref, scaled_ref, weight_ref, own_ref, one_ref, two_ref, three_ref, packed, sems,
-    *, heads, head_dim, tabs
-):
+    tab_ref, scaled_ref, weight_ref, after_ref, *refs, heads, head_dim, tabs, relatives
+):
+    *outs, packed, sems = refs
     spans = [(SMALL, WIDE), (SMALL + WIDE, WIDE)]
-    copies = weight_copies(tab_ref, weight_ref, packed, sems, spans, tabs, heads, head_dim)
+    copies = weight_copies(
+        tab_ref, weight_ref, packed, sems, spans, tabs, heads, head_dim, relatives
+    )
     for copy in copies:
         copy.start()
-    for copy in copies:
-        copy.wait()
     size = 2 * LANES
-    for relative, out in enumerate([own_ref, one_ref, two_ref, three_ref]):
+    each = len(copies) // len(outs)
+    for index, out in enumerate(outs):
+        for copy in copies[index * each : (index + 1) * each]:
+            copy.wait()
         term = lax.dot_general(
-            scaled_ref[...], packed[relative * size : (relative + 1) * size], ROWS_DIMS,
+            scaled_ref[...], packed[index * size : (index + 1) * size], ROWS_DIMS,
             preferred_element_type=jnp.float32,
         )
         out[...] = term.astype(out.dtype)
 
 
-def project(tab_index, scaled, weight, heads, head_dim, tabs):
+def project(tab_index, scaled, weight, after, heads, head_dim, tabs, relatives, dtype):
     length, width = scaled.shape
     size = (length, 2 * LANES)
+    count = len(relatives)
     return pl.pallas_call(
-        lambda *refs: project_kernel(*refs, heads=heads, head_dim=head_dim, tabs=tabs),
-        out_shape=[whole(size, jnp.float32)] + [whole(size, jnp.bfloat16)] * (tabs - 1),
-        in_specs=[SMEM, VMEM, ANY],
-        out_specs=[VMEM] * tabs,
+        lambda *refs: project_kernel(
+            *refs, heads=heads, head_dim=head_dim, tabs=tabs, relatives=relatives
+        ),
+        out_shape=[kept(size, dtype)] * count,
+        in_specs=[SMEM, VMEM, ANY, ANY],
+        out_specs=[VMEM] * count,
         scratch_shapes=[
-            pltpu.VMEM((tabs * 2 * LANES, width), jnp.bfloat16),
-            pltpu.SemaphoreType.DMA((tabs * heads * 2,)),
+            pltpu.VMEM((count * 2 * LANES, width), jnp.bfloat16),
+            pltpu.SemaphoreType.DMA((count * heads * 2,)),
         ],
+        compiler_params=LIMIT,
         name="project",
-    )(tab_index, scaled, weight)
+    )(tab_index, *near(scaled), *far(weight), after)
 
 
 def sort_tokens(place_ref, grads, ordered, tiles):
@@ -327,15 +369,16 @@
     heads, length = places.shape
     return pl.pallas_call(
         send_small_kernel,
-        out_shape=whole((peers, SMALL + META, LANES), jnp.bfloat16),
+        out_shape=kept((peers, SMALL + META, LANES), jnp.bfloat16),
         in_specs=[SMEM] + [VMEM] * 6,
         out_specs=VMEM,
         scratch_shapes=[
             pltpu.VMEM((length, LANES), jnp.bfloat16),
             pltpu.VMEM((heads, 1, length + HALF, LANES), jnp.float32),
         ],
+        compiler_params=LIMIT,
         name="send_small",
-    )(starts, places, meta, terms[0], *near(*terms[1:]))
+    )(starts, places, meta, *near(*terms))
 
 
 def send_wide_kernel(
@@ -365,15 +408,16 @@
     heads, length = places.shape
     return pl.pallas_call(
         send_wide_kernel,
-        out_shape=whole((peers, 2 * HALF, LANES), jnp.bfloat16),
+        out_shape=kept((peers, 2 * HALF, LANES), jnp.bfloat16),
         in_specs=[SMEM] + [VMEM] * 5 + [ANY],
         out_specs=VMEM,
         scratch_shapes=[
             pltpu.VMEM((length, 2 * LANES), jnp.bfloat16),
             pltpu.VMEM((heads, 2, length + HALF, LANES), jnp.float32),
         ],
+        compiler_params=LIMIT,
         name="send_wide",
-    )(starts, places, terms[0], *near(*terms[1:]), after)
+    )(starts, places, *near(*terms), after)
 
 
 def add_small_kernel(got_ref, grad_ref, hits_ref, number_ref, numbers):
@@ -418,19 +462,28 @@
     return pl.pallas_call(
         add_small_kernel,
         out_shape=[
-            whole((heads, SMALL, rows), jnp.float32),
-            whole((heads, 8, rows), jnp.float32),
-            whole((heads, peers // 2, LANES), jnp.int32),
+            kept((heads, SMALL, rows), jnp.float32),
+            kept((heads, 8, rows), jnp.float32),
+            kept((heads, peers // 2, LANES), jnp.int32),
         ],
         scratch_shapes=[pltpu.VMEM((peers, LANES), jnp.float32)],
+        compiler_params=LIMIT,
         name="add_small",
     )(*near(got))
 
 
 def update_kernel(
-    got_ref, small_ref, hits_ref, number_ref, table_ref, one_ref, two_ref,
-    new_table, new_one, new_two
-):
+    got_ref, small_ref, hits_ref, number_ref, table_far, one_far, two_far,
+    new_table, new_one, new_two, table_ref, one_ref, two_ref, sems
+):
+    loads = [
+        pltpu.make_async_copy(source, target, sems.at[index])
+        for index, (source, target) in enumerate(
+            [(table_far, table_ref), (one_far, one_ref), (two_far, two_ref)]
+        )
+    ]
+    for load in loads:
+        load.start()
     peers = got_ref.shape[0]
     heads, head_dim, rows = table_ref.shape
     row_of = lax.broadcasted_iota(jnp.int32, (rows, LANES), 0)
@@ -453,6 +506,8 @@
             totals[h] = totals[h] + jnp.dot(
                 jnp.concatenate(chosen, axis=1), block, preferred_element_type=jnp.float32
             )
+    for load in loads:
+        load.wait()
     left = lane_below(rows, HALF)
     turned = [
         jnp.where(
@@ -479,8 +534,13 @@
     return pl.pallas_call(
         update_kernel,
         out_shape=[whole(table.shape, jnp.float32)] * 3,
+        in_specs=[VMEM] * 4 + [ANY] * 3,
+        out_specs=[VMEM] * 3,
+        scratch_shapes=[pltpu.VMEM(table.shape, jnp.float32)] * 3
+        + [pltpu.SemaphoreType.DMA((3,))],
+        compiler_params=LIMIT,
         name="update",
-    )(*near(got), small, hits, numbers, table, one, two)
+    )(*near(got, small, hits, numbers), *far(table, one, two))
 
 
 def shards(
@@ -503,17 +563,25 @@
     prior = shift_by(saved_value[length - HALO :], "seq", 1, False)
     following = jnp.concatenate([saved_value[:HALO], cotangent[:HALO]], axis=0)
     following = shift_by(following, "seq", -1, False)
-    places, starts, meta = plan(owner_ids[:, :, 0], local_row, peers)
+    places, starts, meta = plan(jnp.swapaxes(owner_ids, 1, 2), local_row, peers)
     scaled, *small = adjoint_terms(
         tab_index, cotangent, saved_value, prior, following, gate_scale.reshape(-1, LANES),
-        conv_weight, value_weight, heads, head_dim, tabs,
+        conv_weight, value_weight, places, heads, head_dim, tabs,
     )
-    wide = list(project(tab_index, scaled, value_weight, heads, head_dim, tabs))
+    sizes = (heads, head_dim, tabs)
+    wide = [None] + list(
+        project(
+            tab_index, scaled, value_weight, tab_index, *sizes, range(1, tabs), jnp.bfloat16
+        )
+    )
     for i in range(1, tabs):
         small[i] = shift_by(small[i], "tab", i, True)
         wide[i] = shift_by(wide[i], "tab", i, True)
     blocks = send_small(starts, places, meta, small, peers)
     got = lax.all_to_all(blocks, "seq", split_axis=0, concat_axis=0, tiled=True)
+    wide[:1] = project(
+        tab_index, scaled, value_weight, blocks, *sizes, range(1), jnp.float32
+    )
     wide_blocks = send_wide(starts, places, wide, blocks, peers)
     wide_got = lax.all_to_all(wide_blocks, "seq", split_axis=0, concat_axis=0, tiled=True)
     small_grad, hits, numbers = add_small(got, heads, rows)

time: 149 us -> 144 us (0.966)
  Pallas kernels: 30.8 us -> 27.2 us
    pallas_call x3, Pallas kernels: 11.3 us -> 9.43 us  [the longest x1 3.83 us: send_wide(): pl.pallas_call(send_wide_kernel, out_shape=kept((peers, 2 * HALF, LANES),...]
    pallas_call x1 -> x2, Pallas kernels: 5.6 us -> 5.38 us  [project(): pl.pallas_call(lambda *refs: project_kernel(*refs, heads=heads, head_dim=...]
  transfers between devices with their start and end apart: 10 -> 10, of which waited for: 5 -> 5; matrix products, arithmetic and copies ran while one was open for 0% -> 0% of each run, Pallas kernels for 10% -> 9%
where the time goes in v3:
time: 144 us
  waiting for transfers between devices  73.8 us (51%)
  starting transfers between devices  40.2 us (28%)
  Pallas kernels  27.2 us (19%)
  local copies, waits for them, and re-layouts  1.48 us (1%)
    all_to_all x1, waiting for transfers between devices, shards(): lax.all_to_all(wide_blocks, 'seq', split_axis=0, concat_axis=0, tiled=True)  48.7 us
    ppermute x8, waiting for transfers between devices, shift_by(): return lax.ppermute(block, axis, route)  25.1 us
    ppermute x8, starting transfers between devices, shift_by(): return lax.ppermute(block, axis, route)  16.3 us
    all_to_all x1, starting transfers between devices, shards(): got = lax.all_to_all(blocks, 'seq', split_axis=0, concat_axis=0, tiled=True)  12.5 us
    all_to_all x1, starting transfers between devices, shards(): lax.all_to_all(wide_blocks, 'seq', split_axis=0, concat_axis=0, tiled=True)  11.4 us
    pallas_call x1, Pallas kernels, updated(): pl.pallas_call(update_kernel, out_shape=[whole(table.shape, jnp.float32)]...  5.5 us
    pallas_call x2, Pallas kernels, project(): pl.pallas_call(lambda *refs: project_kernel(*refs, heads=heads, head_dim=...  5.38 us
    pallas_call x1, Pallas kernels, adjoint_terms(): pl.pallas_call(lambda *refs: adjoint_kernel(*refs, heads=heads, head_dim=...  5.26 us
  transfers between devices with their start and end apart: 10, of which 5 were waited for; matrix products, arithmetic and copies ran while one was open for 0% of the time, Pallas kernels for 9%

profile of v3, /device:TPU:1, one launch (start us, length us, event | category | flops | bytes accessed | tf_op | source)
XLA Modules:
  0.0 143.6 jit_solution(13278570573993609385)
XLA Ops:
  0.6 0.8 fusion
  1.4 0.7 slice.11
  2.1 5.1 %collective-permute-start.1 = (bf16[32,640]{1,0:T(8,128)(2,1)S(1)}, bf16[32,640]{1,0:T(8,128)(2,1)S(1)}, u32[]{:S(2)}, u32[]{:S(2)}) collective-permute-start(bf16[32,640]{1,0:T(8,128)(2,1)S(1)} %pad_maximum_fusion), channel_id=1, source_target_pairs={{4,0},{8,4},{12,8},{16,12},{20,16},{24,20},{28,24},{32,28},{36,32}... | collective-permute-start | bytes 122888 | tf_op jit(solution)/shard_map/ppermute | solution.py:36
  7.2 1.9 %collective-permute-start = (bf16[16,640]{1,0:T(8,128)(2,1)S(1)}, bf16[16,640]{1,0:T(8,128)(2,1)S(1)}, u32[]{:S(2)}, u32[]{:S(2)}) collective-permute-start(bf16[16,640]{1,0:T(8,128)(2,1)S(1)} %get-tuple-element.38), channel_id=1, source_target_pairs={{0,4},{4,8},{8,12},{12,16},{16,20},{20,24},{24,28},{28,32},{32,36}... | collective-permute-start | bytes 61448 | tf_op jit(solution)/shard_map/ppermute | solution.py:36
  9.2 1.6 %plan.1 = (s32[2,1024]{1,0:T(2,128)S(1)}, s32[2,128]{1,0:T(2,128)S(1)}, f32[128,128]{1,0:T(8,128)S(1)}) custom-call(s32[2,1,1024]{2,1,0:T(1,128)} %bitcast.12, s32[2,1024]{1,0:T(2,128)} %refs_1_.2), custom_call_target="tpu_custom_call" | custom-call | tf_op jit(solution)/shard_map/plan/pallas_call | solution.py:113
  10.8 0.0 collective-permute-done.refs_3_
  10.8 0.0 collective-permute-done.1.refs_4_
  10.8 5.3 %adjoint.1 = (bf16[1024,640]{1,0:T(8,128)(2,1)S(1)}, f32[512,128]{1,0:T(8,128)S(1)}, bf16[512,128]{1,0:T(8,128)(2,1)S(1)}, bf16[512,128]{1,0:T(8,128)(2,1)S(1)}, bf16[512,128]{1,0:T(8,128)(2,1)S(1)}) custom-call(s32[1]{0:T(128)} %bitcast.1.refs_0_.refs_3_, bf16[1024,640]{1,0:T(8,128)(2,1)} %refs_1_.3, bf16[1024,640]{1,0:T(8,128)(2,1)} %refs_2_.3, ...), custom_call_target="tpu_custom_call" | custom-call | tf_op jit(solution)/shard_map/adjoint/pallas_call | solution.py:246
  16.1 1.1 collective-permute-start.2
  17.2 2.4 %collective-permute-start.3 = (bf16[512,128]{1,0:T(8,128)(2,1)S(1)}, bf16[512,128]{1,0:T(8,128)(2,1)S(1)}, u32[]{:S(2)}, u32[]{:S(2)}) collective-permute-start(bf16[512,128]{1,0:T(8,128)(2,1)S(1)} %get-tuple-element.26), channel_id=1, source_target_pairs={{0,2},{1,3},{2,0},{3,1},{4,6},{5,7},{6,4},{7,5},{8,10},{9,11},{10,... | collective-permute-start | bytes 393224 | tf_op jit(solution)/shard_map/ppermute | solution.py:36
  19.6 1.2 collective-permute-start.4
  20.8 1.1 collective-permute-done.2.one_ref
  21.9 3.7 %collective-permute-done.3.two_ref = bf16[512,128]{1,0:T(8,128)(2,1)S(1)} collective-permute-done((bf16[512,128]{1,0:T(8,128)(2,1)S(1)}, bf16[512,128]{1,0:T(8,128)(2,1)S(1)}, u32[]{:S(2)}, u32[]{:S(2)}) %collective-permute-start.3) | collective-permute-done | bytes 131104 | tf_op jit(solution)/shard_map/ppermute | solution.py:36
  25.6 0.0 collective-permute-done.4.three_ref
  25.6 3.1 %send_small.1.refs_3_.after_ref = bf16[64,40,128]{2,1,0:T(8,128)(2,1)} custom-call(s32[2,128]{1,0:T(2,128)S(1)} %get-tuple-element.20.start_ref, s32[2,1024]{1,0:T(2,128)S(1)} %get-tuple-element.21.refs_8_.place_ref, f32[128,128]{1,0:T(8,128)S(1)} %get-tuple-element.23.meta_ref, f32[512,128]{1,0:T(8,128)S(1)} %get-tuple-element.24.own_ref, ...), custom_call_target="tpu_custom_call" | custom-call | tf_op jit(solution)/shard_map/send_small/pallas_call | solution.py:370
  28.7 12.5 %all-to-all-start.1 = ((bf16[64,40,128]{2,1,0:T(8,128)(2,1)}), bf16[64,40,128]{2,1,0:T(8,128)(2,1)S(1)}, u32[]{:S(2)}, u32[]{:S(2)}) async-start(bf16[64,40,128]{2,1,0:T(8,128)(2,1)} %send_small.1.refs_3_.after_ref), calls=%async_computation.1 | async-start | bytes 1310720 | tf_op jit(solution)/shard_map/all_to_all | solution.py:581
  41.3 3.7 %project.3 = (bf16[1024,256]{1,0:T(8,128)(2,1)S(1)}, bf16[1024,256]{1,0:T(8,128)(2,1)S(1)}, bf16[1024,256]{1,0:T(8,128)(2,1)S(1)}) custom-call(s32[1]{0:T(128)} %bitcast.1.refs_0_.refs_3_, bf16[1024,640]{1,0:T(8,128)(2,1)S(1)} %get-tuple-element.22.refs_1_, bf16[1280,640]{1,0:T(8,128)(2,1)} %refs_2_.5, s32[1]{0:T(128)} %bitcast.1.refs_0_.refs_3_), custom_call_target="tpu_custom_call" | custom-call | tf_op jit(solution)/shard_map/project/pallas_call | solution.py:293
  45.0 1.5 %collective-permute-start.5 = (bf16[1024,256]{1,0:T(8,128)(2,1)S(1)}, bf16[1024,256]{1,0:T(8,128)(2,1)S(1)}, u32[]{:S(2)}, u32[]{:S(2)}) collective-permute-start(bf16[1024,256]{1,0:T(8,128)(2,1)S(1)} %get-tuple-element.28), channel_id=1, source_target_pairs={{0,1},{1,2},{2,3},{3,0},{4,5},{5,6},{6,7},{7,4},{8,9},{9,10},{10,1... | collective-permute-start | bytes 1572872 | tf_op jit(solution)/shard_map/ppermute | solution.py:36
  46.5 2.1 %collective-permute-start.6 = (bf16[1024,256]{1,0:T(8,128)(2,1)S(1)}, bf16[1024,256]{1,0:T(8,128)(2,1)S(1)}, u32[]{:S(2)}, u32[]{:S(2)}) collective-permute-start(bf16[1024,256]{1,0:T(8,128)(2,1)S(1)} %get-tuple-element.29), channel_id=1, source_target_pairs={{0,2},{1,3},{2,0},{3,1},{4,6},{5,7},{6,4},{7,5},{8,10},{9,11},{10,... | collective-permute-start | bytes 1572872 | tf_op jit(solution)/shard_map/ppermute | solution.py:36
  48.7 0.9 collective-permute-start.7
  49.5 1.6 %project.2.own_ref = f32[1024,256]{1,0:T(8,128)S(1)} custom-call(s32[1]{0:T(128)} %bitcast.1.refs_0_.refs_3_, bf16[1024,640]{1,0:T(8,128)(2,1)S(1)} %get-tuple-element.22.refs_1_, bf16[1280,640]{1,0:T(8,128)(2,1)} %refs_2_.5, bf16[64,40,128]{2,1,0:T(8,128)(2,1)} %send_small.1.refs_3_.after_ref), custom_call_target="tpu_custom_call" | custom-call | tf_op jit(solution)/shard_map/project/pallas_call | solution.py:293
  51.2 8.1 %collective-permute-done.5.one_ref = bf16[1024,256]{1,0:T(8,128)(2,1)S(1)} collective-permute-done((bf16[1024,256]{1,0:T(8,128)(2,1)S(1)}, bf16[1024,256]{1,0:T(8,128)(2,1)S(1)}, u32[]{:S(2)}, u32[]{:S(2)}) %collective-permute-start.5) | collective-permute-done | bytes 524320 | tf_op jit(solution)/shard_map/ppermute | solution.py:36
  59.3 12.1 %collective-permute-done.6.two_ref = bf16[1024,256]{1,0:T(8,128)(2,1)S(1)} collective-permute-done((bf16[1024,256]{1,0:T(8,128)(2,1)S(1)}, bf16[1024,256]{1,0:T(8,128)(2,1)S(1)}, u32[]{:S(2)}, u32[]{:S(2)}) %collective-permute-start.6) | collective-permute-done | bytes 524320 | tf_op jit(solution)/shard_map/ppermute | solution.py:36
  71.5 0.0 collective-permute-done.7.three_ref
  71.5 3.8 %send_wide.1 = bf16[64,128,128]{2,1,0:T(8,128)(2,1)} custom-call(s32[2,128]{1,0:T(2,128)S(1)} %get-tuple-element.20.start_ref, s32[2,1024]{1,0:T(2,128)S(1)} %get-tuple-element.21.refs_8_.place_ref, f32[1024,256]{1,0:T(8,128)S(1)} %project.2.own_ref, bf16[1024,256]{1,0:T(8,128)(2,1)S(1)} %collective-permute-done.5.one_ref, ...), custom_call_target="tpu_custom_call" | custom-call | tf_op jit(solution)/shard_map/send_wide/pallas_call | solution.py:409
  75.3 0.0 all-to-all-done.1.got_ref
  75.3 11.4 %all-to-all-start = ((bf16[64,128,128]{2,1,0:T(8,128)(2,1)}), bf16[64,128,128]{2,1,0:T(8,128)(2,1)S(1)}, u32[]{:S(2)}, u32[]{:S(2)}) async-start(bf16[64,128,128]{2,1,0:T(8,128)(2,1)} %send_wide.1), calls=%async_computation | async-start | bytes 4194304 | tf_op jit(solution)/shard_map/all_to_all | solution.py:586
  86.7 2.5 %add_small.1 = (f32[2,32,512]{2,1,0:T(8,128)S(1)}, f32[2,8,512]{2,1,0:T(8,128)S(1)}, s32[2,32,128]{2,1,0:T(8,128)S(1)}) custom-call(bf16[64,40,128]{2,1,0:T(8,128)(2,1)S(1)} %all-to-all-done.1.got_ref), custom_call_target="tpu_custom_call" | custom-call | tf_op jit(solution)/shard_map/add_small/pallas_call | solution.py:462
  89.2 48.7 %all-to-all-done.got_ref = bf16[64,128,128]{2,1,0:T(8,128)(2,1)S(1)} async-done(((bf16[64,128,128]{2,1,0:T(8,128)(2,1)}), bf16[64,128,128]{2,1,0:T(8,128)(2,1)S(1)}, u32[]{:S(2)}, u32[]{:S(2)}) %all-to-all-start) | async-done | bytes 2097184 | tf_op jit(solution)/shard_map/all_to_all | solution.py:586
  137.9 5.5 %update.1 = (f32[2,160,512]{2,1,0:T(8,128)}, f32[2,160,512]{2,1,0:T(8,128)}, f32[2,160,512]{2,1,0:T(8,128)}) custom-call(bf16[64,128,128]{2,1,0:T(8,128)(2,1)S(1)} %all-to-all-done.got_ref, f32[2,32,512]{2,1,0:T(8,128)S(1)} %get-tuple-element.31.small_ref, f32[2,8,512]{2,1,0:T(8,128)S(1)} %get-tuple-element.32.hits_ref, ...), custom_call_target="tpu_custom_call" | custom-call | tf_op jit(solution)/shard_map/update/pallas_call | solution.py:534
  (1 shorter events, 0.0 us)
Async XLA Ops:
  2.1 8.7 %collective-permute-start.1 = (bf16[32,640]{1,0:T(8,128)(2,1)S(1)}, bf16[32,640]{1,0:T(8,128)(2,1)S(1)}, u32[]{:S(2)}, u32[]{:S(2)}) collective-permute-start(bf16[32,640]{1,0:T(8,128)(2,1)S(1)} %pad_maximum_fusion), channel_id=1, source_target_pairs={{4,0},{8,4},{12,8},{16,12},{20,16},{24,20},{28,24},{32,28},{36,32}... | collective-permute-start | bytes 122888 | tf_op jit(solution)/shard_map/ppermute | solution.py:36
  7.2 3.6 %collective-permute-start = (bf16[16,640]{1,0:T(8,128)(2,1)S(1)}, bf16[16,640]{1,0:T(8,128)(2,1)S(1)}, u32[]{:S(2)}, u32[]{:S(2)}) collective-permute-start(bf16[16,640]{1,0:T(8,128)(2,1)S(1)} %get-tuple-element.38), channel_id=1, source_target_pairs={{0,4},{4,8},{8,12},{12,16},{16,20},{20,24},{24,28},{28,32},{32,36}... | collective-permute-start | bytes 61448 | tf_op jit(solution)/shard_map/ppermute | solution.py:36
  16.1 5.8 %collective-permute-start.2 = (bf16[512,128]{1,0:T(8,128)(2,1)S(1)}, bf16[512,128]{1,0:T(8,128)(2,1)S(1)}, u32[]{:S(2)}, u32[]{:S(2)}) collective-permute-start(bf16[512,128]{1,0:T(8,128)(2,1)S(1)} %get-tuple-element.25), channel_id=1, source_target_pairs={{0,1},{1,2},{2,3},{3,0},{4,5},{5,6},{6,7},{7,4},{8,9},{9,10},{10,1... | collective-permute-start | bytes 393224 | tf_op jit(solution)/shard_map/ppermute | solution.py:36
  17.2 8.4 %collective-permute-start.3 = (bf16[512,128]{1,0:T(8,128)(2,1)S(1)}, bf16[512,128]{1,0:T(8,128)(2,1)S(1)}, u32[]{:S(2)}, u32[]{:S(2)}) collective-permute-start(bf16[512,128]{1,0:T(8,128)(2,1)S(1)} %get-tuple-element.26), channel_id=1, source_target_pairs={{0,2},{1,3},{2,0},{3,1},{4,6},{5,7},{6,4},{7,5},{8,10},{9,11},{10,... | collective-permute-start | bytes 393224 | tf_op jit(solution)/shard_map/ppermute | solution.py:36
  19.6 6.0 %collective-permute-start.4 = (bf16[512,128]{1,0:T(8,128)(2,1)S(1)}, bf16[512,128]{1,0:T(8,128)(2,1)S(1)}, u32[]{:S(2)}, u32[]{:S(2)}) collective-permute-start(bf16[512,128]{1,0:T(8,128)(2,1)S(1)} %get-tuple-element.27), channel_id=1, source_target_pairs={{0,3},{1,0},{2,1},{3,2},{4,7},{5,4},{6,5},{7,6},{8,11},{9,8},{10,9... | collective-permute-start | bytes 393224 | tf_op jit(solution)/shard_map/ppermute | solution.py:36
  28.7 46.5 %all-to-all-start.1 = ((bf16[64,40,128]{2,1,0:T(8,128)(2,1)}), bf16[64,40,128]{2,1,0:T(8,128)(2,1)S(1)}, u32[]{:S(2)}, u32[]{:S(2)}) async-start(bf16[64,40,128]{2,1,0:T(8,128)(2,1)} %send_small.1.refs_3_.after_ref), calls=%async_computation.1 | async-start | bytes 1310720 | tf_op jit(solution)/shard_map/all_to_all | solution.py:581
  45.0 14.3 %collective-permute-start.5 = (bf16[1024,256]{1,0:T(8,128)(2,1)S(1)}, bf16[1024,256]{1,0:T(8,128)(2,1)S(1)}, u32[]{:S(2)}, u32[]{:S(2)}) collective-permute-start(bf16[1024,256]{1,0:T(8,128)(2,1)S(1)} %get-tuple-element.28), channel_id=1, source_target_pairs={{0,1},{1,2},{2,3},{3,0},{4,5},{5,6},{6,7},{7,4},{8,9},{9,10},{10,1... | collective-permute-start | bytes 1572872 | tf_op jit(solution)/shard_map/ppermute | solution.py:36
  46.5 24.9 %collective-permute-start.6 = (bf16[1024,256]{1,0:T(8,128)(2,1)S(1)}, bf16[1024,256]{1,0:T(8,128)(2,1)S(1)}, u32[]{:S(2)}, u32[]{:S(2)}) collective-permute-start(bf16[1024,256]{1,0:T(8,128)(2,1)S(1)} %get-tuple-element.29), channel_id=1, source_target_pairs={{0,2},{1,3},{2,0},{3,1},{4,6},{5,7},{6,4},{7,5},{8,10},{9,11},{10,... | collective-permute-start | bytes 1572872 | tf_op jit(solution)/shard_map/ppermute | solution.py:36
  48.7 22.8 %collective-permute-start.7 = (bf16[1024,256]{1,0:T(8,128)(2,1)S(1)}, bf16[1024,256]{1,0:T(8,128)(2,1)S(1)}, u32[]{:S(2)}, u32[]{:S(2)}) collective-permute-start(bf16[1024,256]{1,0:T(8,128)(2,1)S(1)} %get-tuple-element.30), channel_id=1, source_target_pairs={{0,3},{1,0},{2,1},{3,2},{4,7},{5,4},{6,5},{7,6},{8,11},{9,8},{10,9... | collective-permute-start | bytes 1572872 | tf_op jit(solution)/shard_map/ppermute | solution.py:36
  75.3 62.6 %all-to-all-start = ((bf16[64,128,128]{2,1,0:T(8,128)(2,1)}), bf16[64,128,128]{2,1,0:T(8,128)(2,1)S(1)}, u32[]{:S(2)}, u32[]{:S(2)}) async-start(bf16[64,128,128]{2,1,0:T(8,128)(2,1)} %send_wide.1), calls=%async_computation | async-start | bytes 4194304 | tf_op jit(solution)/shard_map/all_to_all | solution.py:586

commit v4 on v3

--- a/solution.py
+++ b/solution.py
@@ -144,11 +144,59 @@
     return copies
 
 
+def edges_kernel(value_far, cot_far, prior_ref, next_ref, value_ref, cot_ref, sems):
+    length = value_far.shape[0]
+    head, tail = pl.ds(0, HALO), pl.ds(length - HALO, HALO)
+    wide_head, wide_tail = pl.ds(0, 2 * HALO), pl.ds(length - 2 * HALO, 2 * HALO)
+    moves = [
+        (value_far.at[tail], prior_ref),
+        (value_far.at[head], next_ref.at[pl.ds(0, HALO)]),
+        (cot_far.at[head], next_ref.at[pl.ds(HALO, HALO)]),
+        (value_far.at[wide_head], value_ref.at[pl.ds(0, 2 * HALO)]),
+        (value_far.at[wide_tail], value_ref.at[pl.ds(2 * HALO, 2 * HALO)]),
+        (cot_far.at[wide_head], cot_ref.at[pl.ds(0, 2 * HALO)]),
+        (cot_far.at[tail], cot_ref.at[pl.ds(2 * HALO, HALO)]),
+    ]
+    copies = [pltpu.make_async_copy(x, y, sems.at[i]) for i, (x, y) in enumerate(moves)]
+    for copy in copies:
+        copy.start()
+    for copy in copies:
+        copy.wait()
+
+
+def edges(value, cot):
+    width = value.shape[1]
+    return pl.pallas_call(
+        edges_kernel,
+        out_shape=[kept((k * HALO, width), value.dtype) for k in (1, 2, 4, 3)],
+        in_specs=[ANY] * 2,
+        out_specs=[VMEM] * 4,
+        scratch_shapes=[pltpu.SemaphoreType.DMA((7,))],
+        compiler_params=LIMIT,
+        name="edges",
+    )(*far(value, cot))
+
+
+def silu_adjoint(mixed, upstream):
+    squashed = jax.nn.sigmoid(mixed)
+    return upstream * squashed * (1.0 + mixed * (1.0 - squashed))
+
+
+def tap_sum(taps_ref, lanes, read, first):
+    total = first
+    for tap in range(4):
+        term = taps_ref[tap : tap + 1, lanes] * read(3 * tap)
+        total = term if total is None else total + term
+    return total
+
+
+def gate_rows(gate_ref, block):
+    return jnp.broadcast_to(gate_ref[pl.ds(block, 1), :], (LANES, LANES)).T
+
+
 def adjoint_kernel(
-    tab_ref, cot_far, value_far, prior_ref, next_ref, gate_ref, taps_ref, weight_ref, after_ref,
-    scaled, own_ref, one_ref, two_ref, three_ref,
-    cot_ref, value_ref, value_pad, grad_pad, packed, sems, cot_sems, value_sems,
-    *, heads, head_dim, tabs
+    tab_ref, cot_far, value_far, gate_ref, taps_ref, weight_ref, after_ref, scaled, packed,
+    cot_ref, value_ref, value_pad, grad_pad, sems, cot_sems, value_sems, *, heads, head_dim, tabs
 ):
     length, width = cot_ref.shape
     piece = length // PIECES
@@ -168,19 +216,8 @@
     strips = width // LANES
     rows = LANES
     for strip in range(strips):
-        lanes = slice(strip * LANES, (strip + 1) * LANES)
-        value_pad[strip, :HALO] = prior_ref[:, lanes].astype(jnp.float32)
-        value_pad[strip, HALO + length :] = next_ref[:HALO, lanes].astype(jnp.float32)
-
-    def adjoint(strip, start, count, upstream):
-        lanes = slice(strip * LANES, (strip + 1) * LANES)
-        mixed = taps_ref[0:1, lanes] * value_pad[strip, pl.ds(start + HALO, count)]
-        for tap in range(1, 4):
-            mixed = mixed + taps_ref[tap : tap + 1, lanes] * value_pad[
-                strip, pl.ds(start + HALO - 3 * tap, count)
-            ]
-        squashed = jax.nn.sigmoid(mixed)
-        return upstream * squashed * (1.0 + mixed * (1.0 - squashed))
+        value_pad[strip, :HALO] = jnp.zeros((HALO, LANES), jnp.float32)
+        grad_pad[strip, length:] = jnp.zeros((HALO, LANES), jnp.float32)
 
     def first(block, carry):
         start = pl.multiple_of(block * rows, rows)
@@ -190,34 +227,91 @@
                 pl.ds(start, rows), lanes
             ].astype(jnp.float32)
             upstream = cot_ref[pl.ds(start, rows), lanes].astype(jnp.float32)
-            grad_pad[strip, pl.ds(start, rows)] = adjoint(strip, start, rows, upstream)
+            mixed = tap_sum(
+                taps_ref, lanes, lambda back: value_pad[strip, pl.ds(start + HALO - back, rows)], None
+            )
+            grad_pad[strip, pl.ds(start, rows)] = silu_adjoint(mixed, upstream)
         return carry
 
     for index in range(PIECES):
         loads[2 * index].wait()
         loads[2 * index + 1].wait()
         lax.fori_loop(index * (piece // rows), (index + 1) * (piece // rows), first, 0)
-    for strip in range(strips):
-        lanes = slice(strip * LANES, (strip + 1) * LANES)
-        upstream = next_ref[HALO:, lanes].astype(jnp.float32)
-        grad_pad[strip, length:] = adjoint(strip, length, HALO, upstream)
 
     def second(block, carry):
         start = pl.multiple_of(block * rows, rows)
-        gate = jnp.broadcast_to(gate_ref[pl.ds(block, 1), :], (LANES, LANES)).T
+        gate = gate_rows(gate_ref, block)
         for strip in range(strips):
             lanes = slice(strip * LANES, (strip + 1) * LANES)
-            total = cot_ref[pl.ds(start, rows), lanes].astype(jnp.float32)
-            for tap in range(4):
-                total = total + taps_ref[tap : tap + 1, lanes] * grad_pad[
-                    strip, pl.ds(start + 3 * tap, rows)
-                ]
+            upstream = cot_ref[pl.ds(start, rows), lanes].astype(jnp.float32)
+            total = tap_sum(
+                taps_ref, lanes, lambda ahead: grad_pad[strip, pl.ds(start + ahead, rows)], upstream
+            )
             scaled[pl.ds(start, rows), lanes] = (gate * total).astype(jnp.bfloat16)
         return carry
 
     lax.fori_loop(0, length // rows, second, 0)
     for copy in copies:
         copy.wait()
+
+
+def adjoint_inside(tab_index, cot, value, gate, taps, weight, after, heads, head_dim, tabs):
+    length, width = cot.shape
+    strips = width // LANES
+    return pl.pallas_call(
+        lambda *refs: adjoint_kernel(*refs, heads=heads, head_dim=head_dim, tabs=tabs),
+        out_shape=[
+            kept((length, width), jnp.bfloat16),
+            kept((tabs * heads * SMALL, width), jnp.bfloat16),
+        ],
+        in_specs=[SMEM] + [ANY] * 2 + [VMEM] * 2 + [ANY] * 2,
+        out_specs=[VMEM] * 2,
+        scratch_shapes=[
+            pltpu.VMEM((length, width), jnp.bfloat16),
+            pltpu.VMEM((length, width), jnp.bfloat16),
+            pltpu.VMEM((strips, length + HALO, LANES), jnp.float32),
+            pltpu.VMEM((strips, length + HALO, LANES), jnp.float32),
+            pltpu.SemaphoreType.DMA((tabs * heads,)),
+            pltpu.SemaphoreType.DMA((PIECES,)),
+            pltpu.SemaphoreType.DMA((PIECES,)),
+        ],
+        compiler_params=LIMIT,
+        name="adjoint",
+    )(tab_index, *far(cot, value, gate, taps, weight), after)
+
+
+def finish_kernel(
+    inside_ref, packed, prior_ref, next_ref, value_ref, cot_ref, gate_ref, taps_ref,
+    scaled, own_ref, one_ref, two_ref, three_ref, window, grads
+):
+    length, width = scaled.shape
+    strips = width // LANES
+    scaled[...] = inside_ref[...]
+    for side in range(2):
+        gate = gate_rows(gate_ref, side * (length // LANES - 1))
+        gate = gate[:HALO] if side == 0 else gate[LANES - HALO :]
+        place = slice(0, HALO) if side == 0 else slice(length - HALO, length)
+        for strip in range(strips):
+            lanes = slice(strip * LANES, (strip + 1) * LANES)
+            values = [prior_ref[:, lanes], value_ref[: 2 * HALO, lanes]]
+            upstream = cot_ref[: 2 * HALO, lanes]
+            if side == 1:
+                values = [value_ref[2 * HALO :, lanes], next_ref[:HALO, lanes]]
+                upstream = jnp.concatenate(
+                    [cot_ref[2 * HALO :, lanes], next_ref[HALO:, lanes]], axis=0
+                )
+            upstream = upstream.astype(jnp.float32)
+            window[side, strip] = jnp.concatenate(values, axis=0).astype(jnp.float32)
+            mixed = tap_sum(
+                taps_ref, lanes,
+                lambda back: window[side, strip, HALO - back : 3 * HALO - back], None,
+            )
+            grads[side, strip] = silu_adjoint(mixed, upstream)
+            total = tap_sum(
+                taps_ref, lanes, lambda ahead: grads[side, strip, ahead : HALO + ahead],
+                upstream[:HALO],
+            )
+            scaled[place, lanes] = (gate * total).astype(jnp.bfloat16)
     fold = length // 2
     left = lane_below(fold, HALF)
     halves = [
@@ -237,31 +331,23 @@
         outs[2 * tile + 1][...] = odd.astype(outs[2 * tile + 1].dtype)
 
 
-def adjoint_terms(
-    tab_index, cot, value, prior, following, gate, taps, weight, after, heads, head_dim, tabs
-):
-    length, width = cot.shape
+def adjoint_terms(inside, packed, halos, gate, taps, tabs):
+    length, width = inside.shape
     strips = width // LANES
     folded = (length // 2, LANES)
     return pl.pallas_call(
-        lambda *refs: adjoint_kernel(*refs, heads=heads, head_dim=head_dim, tabs=tabs),
+        finish_kernel,
         out_shape=[kept((length, width), jnp.bfloat16), kept(folded, jnp.float32)]
         + [kept(folded, jnp.bfloat16)] * (tabs - 1),
-        in_specs=[SMEM] + [ANY] * 2 + [VMEM] * 4 + [ANY] * 2,
+        in_specs=[VMEM] * 8,
         out_specs=[VMEM] * (tabs + 1),
         scratch_shapes=[
-            pltpu.VMEM((length, width), jnp.bfloat16),
-            pltpu.VMEM((length, width), jnp.bfloat16),
-            pltpu.VMEM((strips, length + 2 * HALO, LANES), jnp.float32),
-            pltpu.VMEM((strips, length + HALO, LANES), jnp.float32),
-            pltpu.VMEM((tabs * heads * SMALL, width), jnp.bfloat16),
-            pltpu.SemaphoreType.DMA((tabs * heads,)),
-            pltpu.SemaphoreType.DMA((PIECES,)),
-            pltpu.SemaphoreType.DMA((PIECES,)),
+            pltpu.VMEM((2, strips, 3 * HALO, LANES), jnp.float32),
+            pltpu.VMEM((2, strips, 2 * HALO, LANES), jnp.float32),
         ],
         compiler_params=LIMIT,
-        name="adjoint",
-    )(tab_index, *far(cot, value), *near(prior, following), *far(gate, taps, weight), after)
+        name="finish",
+    )(*near(inside, packed, *halos), gate, taps)
 
 
 def project_kernel(
@@ -474,7 +560,8 @@
 
 def update_kernel(
     got_ref, small_ref, hits_ref, number_ref, table_far, one_far, two_far,
-    new_table, new_one, new_two, table_ref, one_ref, two_ref, sems
+    table_out, one_out, two_out, table_ref, one_ref, two_ref, new_table, new_one, new_two,
+    sems, out_sems
 ):
     loads = [
         pltpu.make_async_copy(source, target, sems.at[index])
@@ -515,6 +602,7 @@
         ).T
         for t in range(2)
     ]
+    stores = []
     for h in range(heads):
         own = slice(h * HALF, (h + 1) * HALF)
         grad = jnp.concatenate([small_ref[h], turned[0][own], turned[1][own]], axis=0)
@@ -528,6 +616,15 @@
         new_table[h] = jnp.where(touched, old_table - learn_rate * update, old_table)
         new_one[h] = jnp.where(touched, first, old_one)
         new_two[h] = jnp.where(touched, second, old_two)
+        for index, (source, target) in enumerate(
+            [(new_table, table_out), (new_one, one_out), (new_two, two_out)]
+        ):
+            stores.append(
+                pltpu.make_async_copy(source.at[h], target.at[h], out_sems.at[h, index])
+            )
+            stores[-1].start()
+    for store in stores:
+        store.wait()
 
 
 def updated(got, small, hits, numbers, table, one, two):
@@ -535,9 +632,9 @@
         update_kernel,
         out_shape=[whole(table.shape, jnp.float32)] * 3,
         in_specs=[VMEM] * 4 + [ANY] * 3,
-        out_specs=[VMEM] * 3,
-        scratch_shapes=[pltpu.VMEM(table.shape, jnp.float32)] * 3
-        + [pltpu.SemaphoreType.DMA((3,))],
+        out_specs=[ANY] * 3,
+        scratch_shapes=[pltpu.VMEM(table.shape, jnp.float32)] * 6
+        + [pltpu.SemaphoreType.DMA((3,)), pltpu.SemaphoreType.DMA((table.shape[0], 3))],
         compiler_params=LIMIT,
         name="update",
     )(*near(got, small, hits, numbers), *far(table, one, two))
@@ -555,18 +652,21 @@
     moment_one,
     moment_two,
 ):
-    length = cotangent.shape[0]
     heads, rows, head_dim = row_table.shape
     peers = lax.axis_size("seq")
     tabs = lax.axis_size("tab")
     tab_index = lax.axis_index("tab").astype(jnp.int32).reshape(1)
-    prior = shift_by(saved_value[length - HALO :], "seq", 1, False)
-    following = jnp.concatenate([saved_value[:HALO], cotangent[:HALO]], axis=0)
+    prior, following, value_edges, cot_edges = edges(saved_value, cotangent)
+    prior = shift_by(prior, "seq", 1, False)
     following = shift_by(following, "seq", -1, False)
     places, starts, meta = plan(jnp.swapaxes(owner_ids, 1, 2), local_row, peers)
+    gate = gate_scale.reshape(-1, LANES)
+    inside, packed = adjoint_inside(
+        tab_index, cotangent, saved_value, gate, conv_weight, value_weight, places, heads,
+        head_dim, tabs,
+    )
     scaled, *small = adjoint_terms(
-        tab_index, cotangent, saved_value, prior, following, gate_scale.reshape(-1, LANES),
-        conv_weight, value_weight, places, heads, head_dim, tabs,
+        inside, packed, (prior, following, value_edges, cot_edges), gate, conv_weight, tabs
     )
     sizes = (heads, head_dim, tabs)
     wide = [None] + list(

time: 144 us -> 144 us (level)
  local copies, waits for them, and re-layouts: 1.48 us -> 0.01 us
    slice x2 -> x0, local copies, waits for them, and re-layouts: 1.48 us -> none  [shards(): following = jnp.concatenate([saved_value[:HALO], cotangent[:HALO]], axis=0)]
    pallas_call x1 -> x3, Pallas kernels: 5.26 us -> 6.53 us  [the longest x1 4.81 us: adjoint_inside(): pl.pallas_call(lambda *refs: adjoint_kernel(*refs, heads=heads, head_dim=...]
  transfers between devices with their start and end apart: 10 -> 10, of which waited for: 5 -> 5; matrix products, arithmetic and copies ran while one was open for 0% -> 0% of each run, Pallas kernels for 9% -> 13%
where the time goes in v4:
time: 144 us; the launch traced here: 143 us
  waiting for transfers between devices  73.4 us (51%)
  starting transfers between devices  40 us (28%)
  Pallas kernels  28.5 us (20%)
    all_to_all x1, waiting for transfers between devices, shards(): lax.all_to_all(wide_blocks, 'seq', split_axis=0, concat_axis=0, tiled=True)  48.7 us
    ppermute x8, waiting for transfers between devices, shift_by(): return lax.ppermute(block, axis, route)  24.7 us
    ppermute x8, starting transfers between devices, shift_by(): return lax.ppermute(block, axis, route)  16.5 us
    all_to_all x1, starting transfers between devices, shards(): got = lax.all_to_all(blocks, 'seq', split_axis=0, concat_axis=0, tiled=True)  12.2 us
    all_to_all x1, starting transfers between devices, shards(): lax.all_to_all(wide_blocks, 'seq', split_axis=0, concat_axis=0, tiled=True)  11.2 us
    pallas_call x1, Pallas kernels, updated(): pl.pallas_call(update_kernel, out_shape=[whole(table.shape, jnp.float32)]...  5.6 us
    pallas_call x2, Pallas kernels, project(): pl.pallas_call(lambda *refs: project_kernel(*refs, heads=heads, head_dim=...  5.38 us
    pallas_call x1, Pallas kernels, adjoint_inside(): pl.pallas_call(lambda *refs: adjoint_kernel(*refs, heads=heads, head_dim=...  4.81 us
  transfers between devices with their start and end apart: 10, of which 5 were waited for; matrix products, arithmetic and copies ran while one was open for 0% of the time, Pallas kernels for 13%

profile of v4, /device:TPU:1, one launch (start us, length us, event | category | flops | bytes accessed | tf_op | source)
XLA Modules:
  0.0 142.9 jit_solution(4519117756850785977)
XLA Ops:
  0.6 0.9 edges.1
  1.6 5.1 %collective-permute-start.1 = (bf16[32,640]{1,0:T(8,128)(2,1)S(1)}, bf16[32,640]{1,0:T(8,128)(2,1)S(1)}, u32[]{:S(2)}, u32[]{:S(2)}) collective-permute-start(bf16[32,640]{1,0:T(8,128)(2,1)S(1)} %get-tuple-element.31), channel_id=1, source_target_pairs={{4,0},{8,4},{12,8},{16,12},{20,16},{24,20},{28,24},{32,28},{36,32}... | collective-permute-start | bytes 122888 | tf_op jit(solution)/shard_map/ppermute | solution.py:36
  6.7 1.9 %collective-permute-start = (bf16[16,640]{1,0:T(8,128)(2,1)S(1)}, bf16[16,640]{1,0:T(8,128)(2,1)S(1)}, u32[]{:S(2)}, u32[]{:S(2)}) collective-permute-start(bf16[16,640]{1,0:T(8,128)(2,1)S(1)} %get-tuple-element.30), channel_id=1, source_target_pairs={{0,4},{4,8},{8,12},{12,16},{16,20},{20,24},{24,28},{28,32},{32,36}... | collective-permute-start | bytes 61448 | tf_op jit(solution)/shard_map/ppermute | solution.py:36
  8.6 1.6 %plan.1 = (s32[2,1024]{1,0:T(2,128)S(1)}, s32[2,128]{1,0:T(2,128)S(1)}, f32[128,128]{1,0:T(8,128)S(1)}) custom-call(s32[2,1,1024]{2,1,0:T(1,128)} %bitcast.14, s32[2,1024]{1,0:T(2,128)} %refs_1_.2), custom_call_target="tpu_custom_call" | custom-call | tf_op jit(solution)/shard_map/plan/pallas_call | solution.py:113
  10.2 0.0 copy-start
  10.3 0.0 copy-start.1
  10.3 4.8 %adjoint.1 = (bf16[1024,640]{1,0:T(8,128)(2,1)S(1)}, bf16[256,640]{1,0:T(8,128)(2,1)S(1)}) custom-call(s32[1]{0:T(128)} %bitcast.1.refs_0_.refs_3_, bf16[1024,640]{1,0:T(8,128)(2,1)} %cot_far.1, bf16[1024,640]{1,0:T(8,128)(2,1)} %value_far.1, f32[8,128]{1,0:T(8,128)} %bitcast.9, f32[4,640]{1,0:T(4,128)} %taps_ref.1, bf16[1280,640]{1,0:T(8,128)(2,1)} %refs_2_.5, ...), custom_call_target="tpu_custom_call" | custom-call | tf_op jit(solution)/shard_map/adjoint/pallas_call | solution.py:261
  15.1 0.0 collective-permute-done.prior_ref
  15.1 0.0 collective-permute-done.1.next_ref
  15.1 0.0 copy-done
  15.1 0.0 copy-done.1
  15.1 0.8 finish.1
  15.9 1.1 collective-permute-start.2
  17.0 2.5 %collective-permute-start.3 = (bf16[512,128]{1,0:T(8,128)(2,1)S(1)}, bf16[512,128]{1,0:T(8,128)(2,1)S(1)}, u32[]{:S(2)}, u32[]{:S(2)}) collective-permute-start(bf16[512,128]{1,0:T(8,128)(2,1)S(1)} %get-tuple-element.38), channel_id=1, source_target_pairs={{0,2},{1,3},{2,0},{3,1},{4,6},{5,7},{6,4},{7,5},{8,10},{9,11},{10,... | collective-permute-start | bytes 393224 | tf_op jit(solution)/shard_map/ppermute | solution.py:36
  19.5 1.2 collective-permute-start.4
  20.6 1.1 collective-permute-done.2.one_ref
  21.8 3.7 %collective-permute-done.3.two_ref = bf16[512,128]{1,0:T(8,128)(2,1)S(1)} collective-permute-done((bf16[512,128]{1,0:T(8,128)(2,1)S(1)}, bf16[512,128]{1,0:T(8,128)(2,1)S(1)}, u32[]{:S(2)}, u32[]{:S(2)}) %collective-permute-start.3) | collective-permute-done | bytes 131104 | tf_op jit(solution)/shard_map/ppermute | solution.py:36
  25.5 0.0 collective-permute-done.4.three_ref
  25.5 3.1 %send_small.1.refs_3_.after_ref = bf16[64,40,128]{2,1,0:T(8,128)(2,1)} custom-call(s32[2,128]{1,0:T(2,128)S(1)} %get-tuple-element.26.start_ref, s32[2,1024]{1,0:T(2,128)S(1)} %get-tuple-element.27.refs_6_.place_ref, f32[128,128]{1,0:T(8,128)S(1)} %get-tuple-element.35.meta_ref, f32[512,128]{1,0:T(8,128)S(1)} %get-tuple-element.36.own_ref, ...), custom_call_target="tpu_custom_call" | custom-call | tf_op jit(solution)/shard_map/send_small/pallas_call | solution.py:456
  28.6 12.2 %all-to-all-start.1 = ((bf16[64,40,128]{2,1,0:T(8,128)(2,1)}), bf16[64,40,128]{2,1,0:T(8,128)(2,1)S(1)}, u32[]{:S(2)}, u32[]{:S(2)}) async-start(bf16[64,40,128]{2,1,0:T(8,128)(2,1)} %send_small.1.refs_3_.after_ref), calls=%async_computation.1 | async-start | bytes 1310720 | tf_op jit(solution)/shard_map/all_to_all | solution.py:681
  40.9 3.7 %project.3 = (bf16[1024,256]{1,0:T(8,128)(2,1)S(1)}, bf16[1024,256]{1,0:T(8,128)(2,1)S(1)}, bf16[1024,256]{1,0:T(8,128)(2,1)S(1)}) custom-call(s32[1]{0:T(128)} %bitcast.1.refs_0_.refs_3_, bf16[1024,640]{1,0:T(8,128)(2,1)S(1)} %get-tuple-element.34.refs_1_, bf16[1280,640]{1,0:T(8,128)(2,1)} %refs_2_.5, s32[1]{0:T(128)} %bitcast.1.refs_0_.refs_3_), custom_call_target="tpu_custom_call" | custom-call | tf_op jit(solution)/shard_map/project/pallas_call | solution.py:379
  44.6 1.3 collective-permute-start.5
  45.9 2.1 %collective-permute-start.6 = (bf16[1024,256]{1,0:T(8,128)(2,1)S(1)}, bf16[1024,256]{1,0:T(8,128)(2,1)S(1)}, u32[]{:S(2)}, u32[]{:S(2)}) collective-permute-start(bf16[1024,256]{1,0:T(8,128)(2,1)S(1)} %get-tuple-element.41), channel_id=1, source_target_pairs={{0,2},{1,3},{2,0},{3,1},{4,6},{5,7},{6,4},{7,5},{8,10},{9,11},{10,... | collective-permute-start | bytes 1572872 | tf_op jit(solution)/shard_map/ppermute | solution.py:36
  48.1 1.3 collective-permute-start.7
  49.3 1.6 %project.2.own_ref = f32[1024,256]{1,0:T(8,128)S(1)} custom-call(s32[1]{0:T(128)} %bitcast.1.refs_0_.refs_3_, bf16[1024,640]{1,0:T(8,128)(2,1)S(1)} %get-tuple-element.34.refs_1_, bf16[1280,640]{1,0:T(8,128)(2,1)} %refs_2_.5, bf16[64,40,128]{2,1,0:T(8,128)(2,1)} %send_small.1.refs_3_.after_ref), custom_call_target="tpu_custom_call" | custom-call | tf_op jit(solution)/shard_map/project/pallas_call | solution.py:379
  51.0 7.9 %collective-permute-done.5.one_ref = bf16[1024,256]{1,0:T(8,128)(2,1)S(1)} collective-permute-done((bf16[1024,256]{1,0:T(8,128)(2,1)S(1)}, bf16[1024,256]{1,0:T(8,128)(2,1)S(1)}, u32[]{:S(2)}, u32[]{:S(2)}) %collective-permute-start.5) | collective-permute-done | bytes 524320 | tf_op jit(solution)/shard_map/ppermute | solution.py:36
  58.9 11.9 %collective-permute-done.6.two_ref = bf16[1024,256]{1,0:T(8,128)(2,1)S(1)} collective-permute-done((bf16[1024,256]{1,0:T(8,128)(2,1)S(1)}, bf16[1024,256]{1,0:T(8,128)(2,1)S(1)}, u32[]{:S(2)}, u32[]{:S(2)}) %collective-permute-start.6) | collective-permute-done | bytes 524320 | tf_op jit(solution)/shard_map/ppermute | solution.py:36
  70.9 0.0 collective-permute-done.7.three_ref
  70.9 3.8 %send_wide.1 = bf16[64,128,128]{2,1,0:T(8,128)(2,1)} custom-call(s32[2,128]{1,0:T(2,128)S(1)} %get-tuple-element.26.start_ref, s32[2,1024]{1,0:T(2,128)S(1)} %get-tuple-element.27.refs_6_.place_ref, f32[1024,256]{1,0:T(8,128)S(1)} %project.2.own_ref, bf16[1024,256]{1,0:T(8,128)(2,1)S(1)} %collective-permute-done.5.one_ref, ...), custom_call_target="tpu_custom_call" | custom-call | tf_op jit(solution)/shard_map/send_wide/pallas_call | solution.py:495
  74.7 0.0 all-to-all-done.1.got_ref
  74.7 11.2 %all-to-all-start = ((bf16[64,128,128]{2,1,0:T(8,128)(2,1)}), bf16[64,128,128]{2,1,0:T(8,128)(2,1)S(1)}, u32[]{:S(2)}, u32[]{:S(2)}) async-start(bf16[64,128,128]{2,1,0:T(8,128)(2,1)} %send_wide.1), calls=%async_computation | async-start | bytes 4194304 | tf_op jit(solution)/shard_map/all_to_all | solution.py:686
  85.9 2.5 %add_small.1 = (f32[2,32,512]{2,1,0:T(8,128)S(1)}, f32[2,8,512]{2,1,0:T(8,128)S(1)}, s32[2,32,128]{2,1,0:T(8,128)S(1)}) custom-call(bf16[64,40,128]{2,1,0:T(8,128)(2,1)S(1)} %all-to-all-done.1.got_ref), custom_call_target="tpu_custom_call" | custom-call | tf_op jit(solution)/shard_map/add_small/pallas_call | solution.py:548
  88.4 48.7 %all-to-all-done.got_ref = bf16[64,128,128]{2,1,0:T(8,128)(2,1)S(1)} async-done(((bf16[64,128,128]{2,1,0:T(8,128)(2,1)}), bf16[64,128,128]{2,1,0:T(8,128)(2,1)S(1)}, u32[]{:S(2)}, u32[]{:S(2)}) %all-to-all-start) | async-done | bytes 2097184 | tf_op jit(solution)/shard_map/all_to_all | solution.py:686
  137.1 5.6 %update.1 = (f32[2,160,512]{2,1,0:T(8,128)}, f32[2,160,512]{2,1,0:T(8,128)}, f32[2,160,512]{2,1,0:T(8,128)}) custom-call(bf16[64,128,128]{2,1,0:T(8,128)(2,1)S(1)} %all-to-all-done.got_ref, f32[2,32,512]{2,1,0:T(8,128)S(1)} %get-tuple-element.43.small_ref, f32[2,8,512]{2,1,0:T(8,128)S(1)} %get-tuple-element.44.hits_ref, ...), custom_call_target="tpu_custom_call" | custom-call | tf_op jit(solution)/shard_map/update/pallas_call | solution.py:631
Async XLA Ops:
  1.6 13.5 %collective-permute-start.1 = (bf16[32,640]{1,0:T(8,128)(2,1)S(1)}, bf16[32,640]{1,0:T(8,128)(2,1)S(1)}, u32[]{:S(2)}, u32[]{:S(2)}) collective-permute-start(bf16[32,640]{1,0:T(8,128)(2,1)S(1)} %get-tuple-element.31), channel_id=1, source_target_pairs={{4,0},{8,4},{12,8},{16,12},{20,16},{24,20},{28,24},{32,28},{36,32}... | collective-permute-start | bytes 122888 | tf_op jit(solution)/shard_map/ppermute | solution.py:36
  6.7 8.4 %collective-permute-start = (bf16[16,640]{1,0:T(8,128)(2,1)S(1)}, bf16[16,640]{1,0:T(8,128)(2,1)S(1)}, u32[]{:S(2)}, u32[]{:S(2)}) collective-permute-start(bf16[16,640]{1,0:T(8,128)(2,1)S(1)} %get-tuple-element.30), channel_id=1, source_target_pairs={{0,4},{4,8},{8,12},{12,16},{16,20},{20,24},{24,28},{28,32},{32,36}... | collective-permute-start | bytes 61448 | tf_op jit(solution)/shard_map/ppermute | solution.py:36
  10.2 4.9 %copy-start = (f32[4,640]{1,0:T(4,128)S(1)}, f32[4,640]{1,0:T(4,128)}, u32[]{:S(2)}) copy-start(f32[4,640]{1,0:T(4,128)} %taps_ref.1) | copy-start | bytes 30724
  10.3 4.9 %copy-start.1 = (f32[1024]{0:T(1024)S(1)}, f32[1024]{0:T(1024)}, u32[]{:S(2)}) copy-start(f32[1024]{0:T(1024)} %param.12) | copy-start | bytes 12292
  15.9 5.9 %collective-permute-start.2 = (bf16[512,128]{1,0:T(8,128)(2,1)S(1)}, bf16[512,128]{1,0:T(8,128)(2,1)S(1)}, u32[]{:S(2)}, u32[]{:S(2)}) collective-permute-start(bf16[512,128]{1,0:T(8,128)(2,1)S(1)} %get-tuple-element.37), channel_id=1, source_target_pairs={{0,1},{1,2},{2,3},{3,0},{4,5},{5,6},{6,7},{7,4},{8,9},{9,10},{10,1... | collective-permute-start | bytes 393224 | tf_op jit(solution)/shard_map/ppermute | solution.py:36
  17.0 8.4 %collective-permute-start.3 = (bf16[512,128]{1,0:T(8,128)(2,1)S(1)}, bf16[512,128]{1,0:T(8,128)(2,1)S(1)}, u32[]{:S(2)}, u32[]{:S(2)}) collective-permute-start(bf16[512,128]{1,0:T(8,128)(2,1)S(1)} %get-tuple-element.38), channel_id=1, source_target_pairs={{0,2},{1,3},{2,0},{3,1},{4,6},{5,7},{6,4},{7,5},{8,10},{9,11},{10,... | collective-permute-start | bytes 393224 | tf_op jit(solution)/shard_map/ppermute | solution.py:36
  19.5 6.0 %collective-permute-start.4 = (bf16[512,128]{1,0:T(8,128)(2,1)S(1)}, bf16[512,128]{1,0:T(8,128)(2,1)S(1)}, u32[]{:S(2)}, u32[]{:S(2)}) collective-permute-start(bf16[512,128]{1,0:T(8,128)(2,1)S(1)} %get-tuple-element.39), channel_id=1, source_target_pairs={{0,3},{1,0},{2,1},{3,2},{4,7},{5,4},{6,5},{7,6},{8,11},{9,8},{10,9... | collective-permute-start | bytes 393224 | tf_op jit(solution)/shard_map/ppermute | solution.py:36
  28.6 46.1 %all-to-all-start.1 = ((bf16[64,40,128]{2,1,0:T(8,128)(2,1)}), bf16[64,40,128]{2,1,0:T(8,128)(2,1)S(1)}, u32[]{:S(2)}, u32[]{:S(2)}) async-start(bf16[64,40,128]{2,1,0:T(8,128)(2,1)} %send_small.1.refs_3_.after_ref), calls=%async_computation.1 | async-start | bytes 1310720 | tf_op jit(solution)/shard_map/all_to_all | solution.py:681
  44.6 14.3 %collective-permute-start.5 = (bf16[1024,256]{1,0:T(8,128)(2,1)S(1)}, bf16[1024,256]{1,0:T(8,128)(2,1)S(1)}, u32[]{:S(2)}, u32[]{:S(2)}) collective-permute-start(bf16[1024,256]{1,0:T(8,128)(2,1)S(1)} %get-tuple-element.40), channel_id=1, source_target_pairs={{0,1},{1,2},{2,3},{3,0},{4,5},{5,6},{6,7},{7,4},{8,9},{9,10},{10,1... | collective-permute-start | bytes 1572872 | tf_op jit(solution)/shard_map/ppermute | solution.py:36
  45.9 24.9 %collective-permute-start.6 = (bf16[1024,256]{1,0:T(8,128)(2,1)S(1)}, bf16[1024,256]{1,0:T(8,128)(2,1)S(1)}, u32[]{:S(2)}, u32[]{:S(2)}) collective-permute-start(bf16[1024,256]{1,0:T(8,128)(2,1)S(1)} %get-tuple-element.41), channel_id=1, source_target_pairs={{0,2},{1,3},{2,0},{3,1},{4,6},{5,7},{6,4},{7,5},{8,10},{9,11},{10,... | collective-permute-start | bytes 1572872 | tf_op jit(solution)/shard_map/ppermute | solution.py:36
  48.1 22.8 %collective-permute-start.7 = (bf16[1024,256]{1,0:T(8,128)(2,1)S(1)}, bf16[1024,256]{1,0:T(8,128)(2,1)S(1)}, u32[]{:S(2)}, u32[]{:S(2)}) collective-permute-start(bf16[1024,256]{1,0:T(8,128)(2,1)S(1)} %get-tuple-element.42), channel_id=1, source_target_pairs={{0,3},{1,0},{2,1},{3,2},{4,7},{5,4},{6,5},{7,6},{8,11},{9,8},{10,9... | collective-permute-start | bytes 1572872 | tf_op jit(solution)/shard_map/ppermute | solution.py:36
  74.7 62.4 %all-to-all-start = ((bf16[64,128,128]{2,1,0:T(8,128)(2,1)}), bf16[64,128,128]{2,1,0:T(8,128)(2,1)S(1)}, u32[]{:S(2)}, u32[]{:S(2)}) async-start(bf16[64,128,128]{2,1,0:T(8,128)(2,1)} %send_wide.1), calls=%async_computation | async-start | bytes 4194304 | tf_op jit(solution)/shard_map/all_to_all | solution.py:686

commit v5 on v4

--- a/solution.py
+++ b/solution.py
@@ -19,7 +19,6 @@
 META = 8
 PIECES = 4
 SMALL = 32
-WIDE = 64
 ROWS_DIMS = (((1,), (1,)), ((), ()))
 VMEM = pl.BlockSpec(memory_space=pltpu.VMEM)
 SMEM = pl.BlockSpec(memory_space=pltpu.SMEM)
@@ -354,7 +353,7 @@
     tab_ref, scaled_ref, weight_ref, after_ref, *refs, heads, head_dim, tabs, relatives
 ):
     *outs, packed, sems = refs
-    spans = [(SMALL, WIDE), (SMALL + WIDE, WIDE)]
+    spans = [(SMALL, LANES)]
     copies = weight_copies(
         tab_ref, weight_ref, packed, sems, spans, tabs, heads, head_dim, relatives
     )
@@ -455,7 +454,7 @@
     heads, length = places.shape
     return pl.pallas_call(
         send_small_kernel,
-        out_shape=kept((peers, SMALL + META, LANES), jnp.bfloat16),
+        out_shape=whole((peers, SMALL + META, LANES), jnp.bfloat16),
         in_specs=[SMEM] + [VMEM] * 6,
         out_specs=VMEM,
         scratch_shapes=[
@@ -473,18 +472,14 @@
     peers = out_ref.shape[0]
     grads[...] = summed([own_ref, one_ref, two_ref, three_ref], slice(None)).astype(jnp.bfloat16)
     sort_tokens(place_ref, grads, ordered, 2)
-    left = lane_below(HALF, HALF)
     unroll = 2
 
     def body(step, carry):
         for part in range(unroll):
             peer = step * unroll + part
-            for tile in range(2):
-                a = ordered[0, tile, pl.ds(start_ref[0, peer], HALF)]
-                b = ordered[1, tile, pl.ds(start_ref[1, peer], HALF)]
-                out_ref[peer, tile * HALF : (tile + 1) * HALF] = jnp.where(left, a, b).astype(
-                    jnp.bfloat16
-                )
+            for h in range(2):
+                window = ordered[h, h, pl.ds(start_ref[h, peer], HALF)]
+                out_ref[peer, h * HALF : (h + 1) * HALF] = window.astype(jnp.bfloat16)
         return carry
 
     lax.fori_loop(0, peers // unroll, body, 0)
@@ -494,7 +489,7 @@
     heads, length = places.shape
     return pl.pallas_call(
         send_wide_kernel,
-        out_shape=kept((peers, 2 * HALF, LANES), jnp.bfloat16),
+        out_shape=whole((peers, 2 * HALF, LANES), jnp.bfloat16),
         in_specs=[SMEM] + [VMEM] * 5 + [ANY],
         out_specs=VMEM,
         scratch_shapes=[
@@ -506,7 +501,7 @@
     )(starts, places, *near(*terms), after)
 
 
-def add_small_kernel(got_ref, grad_ref, hits_ref, number_ref, numbers):
+def add_small_kernel(got_ref, grad_ref, hits_ref, low_ref, column_ref, numbers, number_ref):
     peers = got_ref.shape[0]
     heads, _, rows = grad_ref.shape
     for peer in range(peers):
@@ -518,6 +513,14 @@
     left = lane_below(pairs, HALF)
     number_ref[0] = jnp.where(left, even, pltpu.roll(odd, HALF, 1)).astype(jnp.int32)
     number_ref[1] = jnp.where(left, pltpu.roll(even, HALF, 1), odd).astype(jnp.int32)
+    half = rows // 2
+    upper = []
+    for h in range(heads):
+        number = number_ref[h]
+        low_ref[h] = jnp.where(number >= half, number - half, number)
+        upper.append(jnp.where(number >= half, 1.0, 0.0))
+    upper.append(jnp.zeros((LANES - heads * pairs, LANES), jnp.float32))
+    column_ref[...] = jnp.concatenate(upper, axis=0).T
     row_of = lax.broadcasted_iota(jnp.int32, (rows, LANES), 0)
     keep = lane_below(SMALL, HALF)
     totals = [jnp.zeros((rows, LANES), jnp.float32) for _ in range(heads)]
@@ -551,15 +554,19 @@
             kept((heads, SMALL, rows), jnp.float32),
             kept((heads, 8, rows), jnp.float32),
             kept((heads, peers // 2, LANES), jnp.int32),
-        ],
-        scratch_shapes=[pltpu.VMEM((peers, LANES), jnp.float32)],
+            kept((LANES, LANES), jnp.float32),
+        ],
+        scratch_shapes=[
+            pltpu.VMEM((peers, LANES), jnp.float32),
+            pltpu.VMEM((heads, peers // 2, LANES), jnp.int32),
+        ],
         compiler_params=LIMIT,
         name="add_small",
     )(*near(got))
 
 
 def update_kernel(
-    got_ref, small_ref, hits_ref, number_ref, table_far, one_far, two_far,
+    got_ref, small_ref, hits_ref, low_ref, column_ref, table_far, one_far, two_far,
     table_out, one_out, two_out, table_ref, one_ref, two_ref, new_table, new_one, new_two,
     sems, out_sems
 ):
@@ -573,39 +580,40 @@
         load.start()
     peers = got_ref.shape[0]
     heads, head_dim, rows = table_ref.shape
-    row_of = lax.broadcasted_iota(jnp.int32, (rows, LANES), 0)
-    totals = [jnp.zeros((rows, 2 * LANES), jnp.float32) for _ in range(heads)]
+    half = rows // 2
+    row_of = lax.broadcasted_iota(jnp.int32, (half, LANES), 0)
+    totals = [jnp.zeros((half, 2 * LANES), jnp.float32) for _ in range(heads)]
     group = 4
     for step in range(peers // group):
-        members = range(step * group, (step + 1) * group)
-        block = jnp.concatenate(
-            [
-                jnp.concatenate([got_ref[peer, :HALF] for peer in members], axis=0),
-                jnp.concatenate([got_ref[peer, HALF:] for peer in members], axis=0),
-            ],
-            axis=1,
-        )
         for h in range(heads):
+            block = jnp.concatenate(
+                [
+                    got_ref[peer, h * HALF : (h + 1) * HALF]
+                    for peer in range(step * group, (step + 1) * group)
+                ],
+                axis=0,
+            )
+            pairs = range(step * group // 2, (step + 1) * group // 2)
+            first = h * (peers // 2)
+            mask = [
+                jnp.broadcast_to(column_ref[:, first + pair : first + pair + 1], (LANES, LANES))
+                for pair in pairs
+            ]
+            upper = block * jnp.concatenate(mask, axis=0).astype(jnp.bfloat16)
+            block = jnp.concatenate([block - upper, upper], axis=1)
             chosen = [
-                ones_where(number_ref[h, 2 * step + i : 2 * step + i + 1] == row_of)
-                for i in range(group // 2)
+                ones_where(low_ref[h, pair : pair + 1] == row_of)
+                for pair in range(step * group // 2, (step + 1) * group // 2)
             ]
             totals[h] = totals[h] + jnp.dot(
                 jnp.concatenate(chosen, axis=1), block, preferred_element_type=jnp.float32
             )
     for load in loads:
         load.wait()
-    left = lane_below(rows, HALF)
-    turned = [
-        jnp.where(
-            left, totals[0][:, t * LANES : (t + 1) * LANES], totals[1][:, t * LANES : (t + 1) * LANES]
-        ).T
-        for t in range(2)
-    ]
     stores = []
     for h in range(heads):
-        own = slice(h * HALF, (h + 1) * HALF)
-        grad = jnp.concatenate([small_ref[h], turned[0][own], turned[1][own]], axis=0)
+        turned = jnp.concatenate([totals[h][:, :LANES].T, totals[h][:, LANES:].T], axis=1)
+        grad = jnp.concatenate([small_ref[h], turned], axis=0)
         touched = jnp.broadcast_to(hits_ref[h, 0:1] > 0.5, (head_dim, rows))
         old_one, old_two, old_table = one_ref[h], two_ref[h], table_ref[h]
         first = beta_one * old_one + (1.0 - beta_one) * grad
@@ -627,17 +635,17 @@
         store.wait()
 
 
-def updated(got, small, hits, numbers, table, one, two):
+def updated(got, small, hits, lows, masks, table, one, two):
     return pl.pallas_call(
         update_kernel,
         out_shape=[whole(table.shape, jnp.float32)] * 3,
-        in_specs=[VMEM] * 4 + [ANY] * 3,
+        in_specs=[VMEM] * 5 + [ANY] * 3,
         out_specs=[ANY] * 3,
         scratch_shapes=[pltpu.VMEM(table.shape, jnp.float32)] * 6
         + [pltpu.SemaphoreType.DMA((3,)), pltpu.SemaphoreType.DMA((table.shape[0], 3))],
         compiler_params=LIMIT,
         name="update",
-    )(*near(got, small, hits, numbers), *far(table, one, two))
+    )(*near(got, small, hits, lows, masks), *far(table, one, two))
 
 
 def shards(
@@ -684,9 +692,9 @@
     )
     wide_blocks = send_wide(starts, places, wide, blocks, peers)
     wide_got = lax.all_to_all(wide_blocks, "seq", split_axis=0, concat_axis=0, tiled=True)
-    small_grad, hits, numbers = add_small(got, heads, rows)
+    small_grad, hits, lows, masks = add_small(got, heads, rows)
     state = [jnp.swapaxes(x, 1, 2) for x in (row_table, moment_one, moment_two)]
-    new = updated(wide_got, small_grad, hits, numbers, *state)
+    new = updated(wide_got, small_grad, hits, lows, masks, *state)
     return tuple(jnp.swapaxes(x, 1, 2) for x in new)
 
 

time: 144 us -> 142 us (0.986)
  no operation moved by 1% of the time
where the time goes in v5:
time: 142 us
  waiting for transfers between devices  73.5 us (52%)
  starting transfers between devices  40 us (28%)
  Pallas kernels  27.1 us (19%)
    all_to_all x1, waiting for transfers between devices, shards(): lax.all_to_all(wide_blocks, 'seq', split_axis=0, concat_axis=0, tiled=True)  48.7 us
    ppermute x8, waiting for transfers between devices, shift_by(): return lax.ppermute(block, axis, route)  24.7 us
    ppermute x8, starting transfers between devices, shift_by(): return lax.ppermute(block, axis, route)  16.5 us
    all_to_all x1, starting transfers between devices, shards(): got = lax.all_to_all(blocks, 'seq', split_axis=0, concat_axis=0, tiled=True)  12.2 us
    all_to_all x1, starting transfers between devices, shards(): lax.all_to_all(wide_blocks, 'seq', split_axis=0, concat_axis=0, tiled=True)  11.2 us
    pallas_call x2, Pallas kernels, project(): pl.pallas_call(lambda *refs: project_kernel(*refs, heads=heads, head_dim=...  5.36 us
    pallas_call x1, Pallas kernels, adjoint_inside(): pl.pallas_call(lambda *refs: adjoint_kernel(*refs, heads=heads, head_dim=...  4.81 us
    pallas_call x1, Pallas kernels, updated(): pl.pallas_call(update_kernel, out_shape=[whole(table.shape, jnp.float32)]...  4.41 us
  transfers between devices with their start and end apart: 10, of which 5 were waited for; matrix products, arithmetic and copies ran while one was open for 0% of the time, Pallas kernels for 13%

profile of v5, /device:TPU:1, one launch (start us, length us, event | category | flops | bytes accessed | tf_op | source)
XLA Modules:
  0.0 141.5 jit_solution(2212697259152490061)
XLA Ops:
  0.6 0.9 edges.1
  1.6 5.1 %collective-permute-start.1 = (bf16[32,640]{1,0:T(8,128)(2,1)S(1)}, bf16[32,640]{1,0:T(8,128)(2,1)S(1)}, u32[]{:S(2)}, u32[]{:S(2)}) collective-permute-start(bf16[32,640]{1,0:T(8,128)(2,1)S(1)} %get-tuple-element.32), channel_id=1, source_target_pairs={{4,0},{8,4},{12,8},{16,12},{20,16},{24,20},{28,24},{32,28},{36,32}... | collective-permute-start | bytes 122888 | tf_op jit(solution)/shard_map/ppermute | solution.py:35
  6.7 1.9 %collective-permute-start = (bf16[16,640]{1,0:T(8,128)(2,1)S(1)}, bf16[16,640]{1,0:T(8,128)(2,1)S(1)}, u32[]{:S(2)}, u32[]{:S(2)}) collective-permute-start(bf16[16,640]{1,0:T(8,128)(2,1)S(1)} %get-tuple-element.31), channel_id=1, source_target_pairs={{0,4},{4,8},{8,12},{12,16},{16,20},{20,24},{24,28},{28,32},{32,36}... | collective-permute-start | bytes 61448 | tf_op jit(solution)/shard_map/ppermute | solution.py:35
  8.6 1.6 %plan.1 = (s32[2,1024]{1,0:T(2,128)S(1)}, s32[2,128]{1,0:T(2,128)S(1)}, f32[128,128]{1,0:T(8,128)S(1)}) custom-call(s32[2,1,1024]{2,1,0:T(1,128)} %bitcast.14, s32[2,1024]{1,0:T(2,128)} %refs_1_.2), custom_call_target="tpu_custom_call" | custom-call | tf_op jit(solution)/shard_map/plan/pallas_call | solution.py:112
  10.2 0.0 copy-start
  10.3 0.0 copy-start.1
  10.3 4.8 %adjoint.1 = (bf16[1024,640]{1,0:T(8,128)(2,1)S(1)}, bf16[256,640]{1,0:T(8,128)(2,1)S(1)}) custom-call(s32[1]{0:T(128)} %bitcast.1.refs_0_.refs_3_, bf16[1024,640]{1,0:T(8,128)(2,1)} %cot_far.1, bf16[1024,640]{1,0:T(8,128)(2,1)} %value_far.1, f32[8,128]{1,0:T(8,128)} %bitcast.9, f32[4,640]{1,0:T(4,128)} %taps_ref.1, bf16[1280,640]{1,0:T(8,128)(2,1)} %refs_2_.5, ...), custom_call_target="tpu_custom_call" | custom-call | tf_op jit(solution)/shard_map/adjoint/pallas_call | solution.py:260
  15.1 0.0 collective-permute-done.prior_ref
  15.1 0.0 collective-permute-done.1.next_ref
  15.1 0.0 copy-done
  15.1 0.0 copy-done.1
  15.1 0.8 finish.1
  15.9 1.1 collective-permute-start.2
  17.0 2.5 %collective-permute-start.3 = (bf16[512,128]{1,0:T(8,128)(2,1)S(1)}, bf16[512,128]{1,0:T(8,128)(2,1)S(1)}, u32[]{:S(2)}, u32[]{:S(2)}) collective-permute-start(bf16[512,128]{1,0:T(8,128)(2,1)S(1)} %get-tuple-element.39), channel_id=1, source_target_pairs={{0,2},{1,3},{2,0},{3,1},{4,6},{5,7},{6,4},{7,5},{8,10},{9,11},{10,... | collective-permute-start | bytes 393224 | tf_op jit(solution)/shard_map/ppermute | solution.py:35
  19.5 1.2 collective-permute-start.4
  20.6 1.1 collective-permute-done.2.one_ref
  21.8 3.7 %collective-permute-done.3.two_ref = bf16[512,128]{1,0:T(8,128)(2,1)S(1)} collective-permute-done((bf16[512,128]{1,0:T(8,128)(2,1)S(1)}, bf16[512,128]{1,0:T(8,128)(2,1)S(1)}, u32[]{:S(2)}, u32[]{:S(2)}) %collective-permute-start.3) | collective-permute-done | bytes 131104 | tf_op jit(solution)/shard_map/ppermute | solution.py:35
  25.5 0.0 collective-permute-done.4.three_ref
  25.5 3.1 %send_small.1.refs_3_.after_ref = bf16[64,40,128]{2,1,0:T(8,128)(2,1)} custom-call(s32[2,128]{1,0:T(2,128)S(1)} %get-tuple-element.27.start_ref, s32[2,1024]{1,0:T(2,128)S(1)} %get-tuple-element.28.refs_6_.place_ref, f32[128,128]{1,0:T(8,128)S(1)} %get-tuple-element.36.meta_ref, f32[512,128]{1,0:T(8,128)S(1)} %get-tuple-element.37.own_ref, ...), custom_call_target="tpu_custom_call" | custom-call | tf_op jit(solution)/shard_map/send_small/pallas_call | solution.py:455
  28.6 12.2 %all-to-all-start.1 = ((bf16[64,40,128]{2,1,0:T(8,128)(2,1)}), bf16[64,40,128]{2,1,0:T(8,128)(2,1)S(1)}, u32[]{:S(2)}, u32[]{:S(2)}) async-start(bf16[64,40,128]{2,1,0:T(8,128)(2,1)} %send_small.1.refs_3_.after_ref), calls=%async_computation.1 | async-start | bytes 1310720 | tf_op jit(solution)/shard_map/all_to_all | solution.py:689
  40.9 3.7 %project.3 = (bf16[1024,256]{1,0:T(8,128)(2,1)S(1)}, bf16[1024,256]{1,0:T(8,128)(2,1)S(1)}, bf16[1024,256]{1,0:T(8,128)(2,1)S(1)}) custom-call(s32[1]{0:T(128)} %bitcast.1.refs_0_.refs_3_, bf16[1024,640]{1,0:T(8,128)(2,1)S(1)} %get-tuple-element.35.refs_1_, bf16[1280,640]{1,0:T(8,128)(2,1)} %refs_2_.5, s32[1]{0:T(128)} %bitcast.1.refs_0_.refs_3_), custom_call_target="tpu_custom_call" | custom-call | tf_op jit(solution)/shard_map/project/pallas_call | solution.py:378
  44.6 1.3 collective-permute-start.5
  45.9 2.1 %collective-permute-start.6 = (bf16[1024,256]{1,0:T(8,128)(2,1)S(1)}, bf16[1024,256]{1,0:T(8,128)(2,1)S(1)}, u32[]{:S(2)}, u32[]{:S(2)}) collective-permute-start(bf16[1024,256]{1,0:T(8,128)(2,1)S(1)} %get-tuple-element.42), channel_id=1, source_target_pairs={{0,2},{1,3},{2,0},{3,1},{4,6},{5,7},{6,4},{7,5},{8,10},{9,11},{10,... | collective-permute-start | bytes 1572872 | tf_op jit(solution)/shard_map/ppermute | solution.py:35
  48.0 1.3 collective-permute-start.7
  49.3 1.6 %project.2.own_ref = f32[1024,256]{1,0:T(8,128)S(1)} custom-call(s32[1]{0:T(128)} %bitcast.1.refs_0_.refs_3_, bf16[1024,640]{1,0:T(8,128)(2,1)S(1)} %get-tuple-element.35.refs_1_, bf16[1280,640]{1,0:T(8,128)(2,1)} %refs_2_.5, bf16[64,40,128]{2,1,0:T(8,128)(2,1)} %send_small.1.refs_3_.after_ref), custom_call_target="tpu_custom_call" | custom-call | tf_op jit(solution)/shard_map/project/pallas_call | solution.py:378
  51.0 7.9 %collective-permute-done.5.one_ref = bf16[1024,256]{1,0:T(8,128)(2,1)S(1)} collective-permute-done((bf16[1024,256]{1,0:T(8,128)(2,1)S(1)}, bf16[1024,256]{1,0:T(8,128)(2,1)S(1)}, u32[]{:S(2)}, u32[]{:S(2)}) %collective-permute-start.5) | collective-permute-done | bytes 524320 | tf_op jit(solution)/shard_map/ppermute | solution.py:35
  58.9 11.9 %collective-permute-done.6.two_ref = bf16[1024,256]{1,0:T(8,128)(2,1)S(1)} collective-permute-done((bf16[1024,256]{1,0:T(8,128)(2,1)S(1)}, bf16[1024,256]{1,0:T(8,128)(2,1)S(1)}, u32[]{:S(2)}, u32[]{:S(2)}) %collective-permute-start.6) | collective-permute-done | bytes 524320 | tf_op jit(solution)/shard_map/ppermute | solution.py:35
  70.8 0.0 collective-permute-done.7.three_ref
  70.8 3.6 %send_wide.1 = bf16[64,128,128]{2,1,0:T(8,128)(2,1)} custom-call(s32[2,128]{1,0:T(2,128)S(1)} %get-tuple-element.27.start_ref, s32[2,1024]{1,0:T(2,128)S(1)} %get-tuple-element.28.refs_6_.place_ref, f32[1024,256]{1,0:T(8,128)S(1)} %project.2.own_ref, bf16[1024,256]{1,0:T(8,128)(2,1)S(1)} %collective-permute-done.5.one_ref, ...), custom_call_target="tpu_custom_call" | custom-call | tf_op jit(solution)/shard_map/send_wide/pallas_call | solution.py:490
  74.5 0.0 all-to-all-done.1.got_ref
  74.5 11.2 %all-to-all-start = ((bf16[64,128,128]{2,1,0:T(8,128)(2,1)}), bf16[64,128,128]{2,1,0:T(8,128)(2,1)S(1)}, u32[]{:S(2)}, u32[]{:S(2)}) async-start(bf16[64,128,128]{2,1,0:T(8,128)(2,1)} %send_wide.1), calls=%async_computation | async-start | bytes 4194304 | tf_op jit(solution)/shard_map/all_to_all | solution.py:694
  85.7 2.5 %add_small.1 = (f32[2,32,512]{2,1,0:T(8,128)S(1)}, f32[2,8,512]{2,1,0:T(8,128)S(1)}, s32[2,32,128]{2,1,0:T(8,128)S(1)}, f32[128,128]{1,0:T(8,128)S(1)}) custom-call(bf16[64,40,128]{2,1,0:T(8,128)(2,1)S(1)} %all-to-all-done.1.got_ref), custom_call_target="tpu_custom_call" | custom-call | tf_op jit(solution)/shard_map/add_small/pallas_call | solution.py:551
  88.2 48.7 %all-to-all-done.got_ref = bf16[64,128,128]{2,1,0:T(8,128)(2,1)S(1)} async-done(((bf16[64,128,128]{2,1,0:T(8,128)(2,1)}), bf16[64,128,128]{2,1,0:T(8,128)(2,1)S(1)}, u32[]{:S(2)}, u32[]{:S(2)}) %all-to-all-start) | async-done | bytes 2097184 | tf_op jit(solution)/shard_map/all_to_all | solution.py:694
  136.9 4.4 %update.1 = (f32[2,160,512]{2,1,0:T(8,128)}, f32[2,160,512]{2,1,0:T(8,128)}, f32[2,160,512]{2,1,0:T(8,128)}) custom-call(bf16[64,128,128]{2,1,0:T(8,128)(2,1)S(1)} %all-to-all-done.got_ref, f32[2,32,512]{2,1,0:T(8,128)S(1)} %get-tuple-element.44.small_ref, f32[2,8,512]{2,1,0:T(8,128)S(1)} %get-tuple-element.45.hits_ref, ...), custom_call_target="tpu_custom_call" | custom-call | tf_op jit(solution)/shard_map/update/pallas_call | solution.py:639
Async XLA Ops:
  1.6 13.5 %collective-permute-start.1 = (bf16[32,640]{1,0:T(8,128)(2,1)S(1)}, bf16[32,640]{1,0:T(8,128)(2,1)S(1)}, u32[]{:S(2)}, u32[]{:S(2)}) collective-permute-start(bf16[32,640]{1,0:T(8,128)(2,1)S(1)} %get-tuple-element.32), channel_id=1, source_target_pairs={{4,0},{8,4},{12,8},{16,12},{20,16},{24,20},{28,24},{32,28},{36,32}... | collective-permute-start | bytes 122888 | tf_op jit(solution)/shard_map/ppermute | solution.py:35
  6.7 8.4 %collective-permute-start = (bf16[16,640]{1,0:T(8,128)(2,1)S(1)}, bf16[16,640]{1,0:T(8,128)(2,1)S(1)}, u32[]{:S(2)}, u32[]{:S(2)}) collective-permute-start(bf16[16,640]{1,0:T(8,128)(2,1)S(1)} %get-tuple-element.31), channel_id=1, source_target_pairs={{0,4},{4,8},{8,12},{12,16},{16,20},{20,24},{24,28},{28,32},{32,36}... | collective-permute-start | bytes 61448 | tf_op jit(solution)/shard_map/ppermute | solution.py:35
  10.2 4.9 %copy-start = (f32[4,640]{1,0:T(4,128)S(1)}, f32[4,640]{1,0:T(4,128)}, u32[]{:S(2)}) copy-start(f32[4,640]{1,0:T(4,128)} %taps_ref.1) | copy-start | bytes 30724
  10.3 4.9 %copy-start.1 = (f32[1024]{0:T(1024)S(1)}, f32[1024]{0:T(1024)}, u32[]{:S(2)}) copy-start(f32[1024]{0:T(1024)} %param.12) | copy-start | bytes 12292
  15.9 5.9 %collective-permute-start.2 = (bf16[512,128]{1,0:T(8,128)(2,1)S(1)}, bf16[512,128]{1,0:T(8,128)(2,1)S(1)}, u32[]{:S(2)}, u32[]{:S(2)}) collective-permute-start(bf16[512,128]{1,0:T(8,128)(2,1)S(1)} %get-tuple-element.38), channel_id=1, source_target_pairs={{0,1},{1,2},{2,3},{3,0},{4,5},{5,6},{6,7},{7,4},{8,9},{9,10},{10,1... | collective-permute-start | bytes 393224 | tf_op jit(solution)/shard_map/ppermute | solution.py:35
  17.0 8.4 %collective-permute-start.3 = (bf16[512,128]{1,0:T(8,128)(2,1)S(1)}, bf16[512,128]{1,0:T(8,128)(2,1)S(1)}, u32[]{:S(2)}, u32[]{:S(2)}) collective-permute-start(bf16[512,128]{1,0:T(8,128)(2,1)S(1)} %get-tuple-element.39), channel_id=1, source_target_pairs={{0,2},{1,3},{2,0},{3,1},{4,6},{5,7},{6,4},{7,5},{8,10},{9,11},{10,... | collective-permute-start | bytes 393224 | tf_op jit(solution)/shard_map/ppermute | solution.py:35
  19.5 6.0 %collective-permute-start.4 = (bf16[512,128]{1,0:T(8,128)(2,1)S(1)}, bf16[512,128]{1,0:T(8,128)(2,1)S(1)}, u32[]{:S(2)}, u32[]{:S(2)}) collective-permute-start(bf16[512,128]{1,0:T(8,128)(2,1)S(1)} %get-tuple-element.40), channel_id=1, source_target_pairs={{0,3},{1,0},{2,1},{3,2},{4,7},{5,4},{6,5},{7,6},{8,11},{9,8},{10,9... | collective-permute-start | bytes 393224 | tf_op jit(solution)/shard_map/ppermute | solution.py:35
  28.6 45.9 %all-to-all-start.1 = ((bf16[64,40,128]{2,1,0:T(8,128)(2,1)}), bf16[64,40,128]{2,1,0:T(8,128)(2,1)S(1)}, u32[]{:S(2)}, u32[]{:S(2)}) async-start(bf16[64,40,128]{2,1,0:T(8,128)(2,1)} %send_small.1.refs_3_.after_ref), calls=%async_computation.1 | async-start | bytes 1310720 | tf_op jit(solution)/shard_map/all_to_all | solution.py:689
  44.6 14.3 %collective-permute-start.5 = (bf16[1024,256]{1,0:T(8,128)(2,1)S(1)}, bf16[1024,256]{1,0:T(8,128)(2,1)S(1)}, u32[]{:S(2)}, u32[]{:S(2)}) collective-permute-start(bf16[1024,256]{1,0:T(8,128)(2,1)S(1)} %get-tuple-element.41), channel_id=1, source_target_pairs={{0,1},{1,2},{2,3},{3,0},{4,5},{5,6},{6,7},{7,4},{8,9},{9,10},{10,1... | collective-permute-start | bytes 1572872 | tf_op jit(solution)/shard_map/ppermute | solution.py:35
  45.9 24.9 %collective-permute-start.6 = (bf16[1024,256]{1,0:T(8,128)(2,1)S(1)}, bf16[1024,256]{1,0:T(8,128)(2,1)S(1)}, u32[]{:S(2)}, u32[]{:S(2)}) collective-permute-start(bf16[1024,256]{1,0:T(8,128)(2,1)S(1)} %get-tuple-element.42), channel_id=1, source_target_pairs={{0,2},{1,3},{2,0},{3,1},{4,6},{5,7},{6,4},{7,5},{8,10},{9,11},{10,... | collective-permute-start | bytes 1572872 | tf_op jit(solution)/shard_map/ppermute | solution.py:35
  48.0 22.8 %collective-permute-start.7 = (bf16[1024,256]{1,0:T(8,128)(2,1)S(1)}, bf16[1024,256]{1,0:T(8,128)(2,1)S(1)}, u32[]{:S(2)}, u32[]{:S(2)}) collective-permute-start(bf16[1024,256]{1,0:T(8,128)(2,1)S(1)} %get-tuple-element.43), channel_id=1, source_target_pairs={{0,3},{1,0},{2,1},{3,2},{4,7},{5,4},{6,5},{7,6},{8,11},{9,8},{10,9... | collective-permute-start | bytes 1572872 | tf_op jit(solution)/shard_map/ppermute | solution.py:35
  74.5 62.5 %all-to-all-start = ((bf16[64,128,128]{2,1,0:T(8,128)(2,1)}), bf16[64,128,128]{2,1,0:T(8,128)(2,1)S(1)}, u32[]{:S(2)}, u32[]{:S(2)}) async-start(bf16[64,128,128]{2,1,0:T(8,128)(2,1)} %send_wide.1), calls=%async_computation | async-start | bytes 4194304 | tf_op jit(solution)/shard_map/all_to_all | solution.py:694
